TPU v7x, 32 devices: a whole 2x2x4 slice. The times are simulated.
32 devices in a mesh: dp: 16 (over z, x, core), tensor: 2 (over y).
Axes of the slice: x: 2, y: 2, z: 4, core: 2. Of those that a mesh axis runs over, the one named last changes fastest.
Arguments:
- tokens: bfloat16 [32, 512, 768], P('dp', 'tensor'), may hold values from -6 to 6
- cotangent: bfloat16 [32, 512, 768], P('dp', 'tensor'), may hold values from -6 to 6
- lengths: int32 [32], replicated, may hold values from 1 to 512, 10240 in all
- slot_order: int32 [32], replicated, may hold values from 0 to 31, each once
- query_weight: bfloat16 [768, 768], P('dp', 'tensor'), may hold values from -0.21875 to 0.21875
- key_weight: bfloat16 [768, 768], P('dp', 'tensor'), may hold values from -0.21875 to 0.21875
- value_weight: bfloat16 [768, 768], P('dp', 'tensor'), may hold values from -0.21875 to 0.21875
- out_weight: bfloat16 [768, 768], P('dp', 'tensor'), may hold values from -1.5 to 1.5
- up_weight: bfloat16 [768, 3072], P('dp', 'tensor'), may hold values from -0.21875 to 0.21875
- down_weight: bfloat16 [768, 3072], P('dp', 'tensor'), may hold values from -0.109375 to 0.109375
- query_bias: float32 [768], P('tensor'), may hold values from -3 to 3
- value_bias: float32 [768], P('tensor'), may hold values from -0.3 to 0.3
- out_bias: float32 [768], replicated, may hold values from -3 to 3
- up_bias: float32 [3072], P('tensor'), may hold values from -3 to 3
- down_bias: float32 [768], replicated, may hold values from -3 to 3
- first_gain: float32 [768], replicated, may hold values from 0.5 to 1.5
- first_offset: float32 [768], replicated, may hold values from -3 to 3
- second_gain: float32 [768], replicated, may hold values from 0.5 to 1.5
- second_offset: float32 [768], replicated, may hold values from -3 to 3
Outputs:
- layer_out: bfloat16 [32, 512, 768], P('dp', 'tensor')
- input_grad: bfloat16 [32, 512, 768], P('dp', 'tensor')
- query_weight_grad: float32 [768, 768], P('dp', 'tensor')
- key_weight_grad: float32 [768, 768], P('dp', 'tensor')
- value_weight_grad: float32 [768, 768], P('dp', 'tensor')
- out_weight_grad: float32 [768, 768], P('dp', 'tensor')
- up_weight_grad: float32 [768, 3072], P('dp', 'tensor')
- down_weight_grad: float32 [768, 3072], P('dp', 'tensor')
- query_bias_grad: float32 [768], P('tensor')
- value_bias_grad: float32 [768], P('tensor')
- out_bias_grad: float32 [768], replicated
- up_bias_grad: float32 [3072], P('tensor')
- down_bias_grad: float32 [768], replicated
- first_gain_grad: float32 [768], replicated
- first_offset_grad: float32 [768], replicated
- second_gain_grad: float32 [768], replicated
- second_offset_grad: float32 [768], replicated
Inputs may be any that keep to these rules, and one draw needn't show every extreme that they name: The lengths of the 32 sequences sum to 10240, and the longest is exactly 512. `slot_order`: every sequence is held by exactly one slot.
All inputs are finite; a program needn't handle non-finite values.
Results may differ from a plain program's by a relative error of at most 0.017.
Values may be sent and summed in bfloat16 or wider, within the bound.
No kernel may reach another device: no remote copies, remote signals or barrier semaphores. Data moves between devices by JAX's collectives and lax.ppermute only.
A program may use at most 128 MiB of HBM per device.

v0:
```python
import functools

import jax
import jax.numpy as jnp
from jax import lax
from jax.experimental import pallas as pl
from jax.experimental.pallas import tpu as pltpu
from jax.sharding import PartitionSpec as P

HEAD = 64
PAIR = 2 * HEAD
EPSILON = 1e-05
SQRT_HALF = 0.7071067811865476
INV_ROOT_TWO_PI = 0.3989422804014327
BOTH = ("dp", "tensor")
F32 = jnp.float32
BF16 = jnp.bfloat16
TILE = 768
ROWS = 128
HBM = pl.BlockSpec(memory_space=pltpu.HBM)
VMEM = pl.BlockSpec(memory_space=pltpu.VMEM)
SMEM = pl.BlockSpec(memory_space=pltpu.SMEM)
LEN, AT_Z, AT_X, AT_C, AT_Y = range(5)
Y_BIT, C_BIT, X_BIT, Z_BIT = 1, 2, 4, 8


def dot_nn(a, b):
    return lax.dot_general(a, b, (((1,), (0,)), ((), ())), preferred_element_type=F32)


def dot_nt(a, b):
    return lax.dot_general(a, b, (((1,), (1,)), ((), ())), preferred_element_type=F32)


def dot_tn(a, b):
    return lax.dot_general(a, b, (((0,), (0,)), ((), ())), preferred_element_type=F32)


def params(mib):
    return pltpu.CompilerParams(vmem_limit_bytes=mib << 20)


def cost(us):
    return pl.CostEstimate(flops=int(us * 2e7), bytes_accessed=int(us * 6e4), transcendentals=0)


def tie(*values):
    return lax.optimization_barrier(values)


def exchange(value, mask):
    count = lax.axis_size("dp") * lax.axis_size("tensor")
    return lax.ppermute(value, BOTH, [(i, i ^ mask) for i in range(count)])


def in_order(bit_at, mine, other, axis=0):
    low = jnp.where(bit_at == 0, mine, other)
    high = jnp.where(bit_at == 0, other, mine)
    return jnp.stack([low, high], axis=axis)


class Gather:
    def __init__(self, first, second, places):
        self.places = places
        self.a, self.b = first, second

    def along_z(self):
        both = jnp.stack([self.a, self.b])
        self.both = both
        self.got = [exchange(both, m * Z_BIT) for m in (1, 2, 3)]

    def first_side(self):
        at_z = self.places[0]
        both, (g1, g2, g3) = self.both, self.got
        rows = []
        for z in range(4):
            far = jnp.where(at_z == z ^ 2, g2, g3)
            rows.append(jnp.where(at_z == z, both, jnp.where(at_z == z ^ 1, g1, far)))
        self.a = jnp.stack([r[0] for r in rows])
        self.b = jnp.stack([r[1] for r in rows])
        self.got = exchange(self.a, X_BIT), exchange(self.b, Y_BIT)

    def second_side(self):
        _, at_x, _, at_y = self.places
        self.a = in_order(at_x, self.a, self.got[0])
        self.b = in_order(at_y, self.b, self.got[1])
        self.got = exchange(self.a, Y_BIT), exchange(self.b, X_BIT)
        self.near = exchange(self.a, C_BIT), exchange(self.b, C_BIT)

    def core(self):
        self.far = exchange(self.got[0], C_BIT), exchange(self.got[1], C_BIT)

    def pieces(self):
        return (
            [self.a, self.near[0], self.got[0], self.far[0]],
            [self.b, self.near[1], self.got[1], self.far[1]],
        )


class Mover:
    def __init__(self, sems):
        self.sems, self.used = sems, 0

    def __call__(self, src, dst):
        copy = pltpu.make_async_copy(src, dst, self.sems.at[self.used])
        self.used += 1
        copy.start()
        return copy


def wait(copies):
    for c in copies:
        c.wait()


def load_pieces(move, scalars, pieces, weight, second, spans):
    copies = []
    for number, piece in enumerate(pieces):
        far, other = number // 2, number % 2
        at_c = scalars[AT_C] ^ other
        for inner in range(2):
            if second:
                at_x, at_y = scalars[AT_X] ^ far, inner
            else:
                at_x, at_y = inner, scalars[AT_Y] ^ far
            for start, width, to in spans:
                column = pl.multiple_of(to(at_y), 128)
                copies.append(
                    move(
                        piece.at[inner, :, :, pl.ds(start, width)],
                        weight.at[:, at_x, at_c, :, pl.ds(column, width)],
                    )
                )
    return copies


def load_whole(move, scalars, pieces, weight, second, spans):
    return [
        move(pieces[0].at[:, :, :, :, pl.ds(start, width)], weight.at[:, :, :, :, pl.ds(to, width)])
        for start, width, to in spans
    ]


def flat(weight):
    return weight.reshape(-1, weight.shape[-1])


def normalize(z):
    mean = jnp.mean(z, axis=-1, keepdims=True)
    center = z - mean
    rscale = lax.rsqrt(jnp.mean(center * center, axis=-1, keepdims=True) + EPSILON)
    return center * rscale, rscale


def norm_backward(e, normal, rscale, gain):
    scaled = e * gain
    mean = jnp.mean(scaled, axis=-1, keepdims=True)
    tilt = jnp.mean(scaled * normal, axis=-1, keepdims=True)
    return rscale * (scaled - mean - normal * tilt)


def column_sum(value):
    return jnp.sum(value, axis=0, keepdims=True)


def odd_lanes(shape):
    return lax.broadcasted_iota(jnp.int32, shape, len(shape) - 1) >= HEAD


def of_head(value, odd):
    mask = odd_lanes(value.shape)
    zero = jnp.zeros_like(value)
    return jnp.where(mask, value, zero) if odd else jnp.where(mask, zero, value)


def pair_of(t):
    return pl.ds(pl.multiple_of(t * PAIR, PAIR), PAIR)


def load_tokens(move, scalars, tokens, other, x):
    half = other.shape[0]
    at = scalars[AT_Y]
    return [
        move(tokens.at[at], x.at[pl.ds(pl.multiple_of(at * half, half), half)]),
        move(other, x.at[pl.ds(pl.multiple_of((1 - at) * half, half), half)]),
    ]


def attend_kernel(load, scalars, tokens, other, vec, *refs):
    first, second, outs, scratch = refs
    move = Mover(scratch[-1])
    x, q, k, v, att, lse, normal, rscale, low, acc, w5 = scratch[:-1]
    copies = load_tokens(move, scalars, tokens, other, x)
    for copy_set in (load[0](move, scalars, first, w5), load[1](move, scalars, second, w5)):
        copies += copy_set
    wait(copies)
    w = flat(w5)
    seq, features = x.shape
    live = lax.broadcasted_iota(jnp.int32, (1, seq), 1) < scalars[LEN]
    scale = HEAD**-0.5
    at_q, at_k, at_v, at_o = (pl.ds(n * features, features) for n in range(4))
    q[...] = ((dot_nn(x[...], w[:, at_q]) + vec[0:1, :]).astype(BF16).astype(F32) * scale).astype(BF16)
    k[...] = dot_nn(x[...], w[:, at_k]).astype(BF16)
    v[...] = (dot_nn(x[...], w[:, at_v]) + vec[1:2, :]).astype(BF16)
    sent = [move(s, o) for s, o in zip((q, k, v), outs[:3])]
    lse[...] = jnp.zeros_like(lse)

    @pl.loop(0, features // PAIR)
    def _(pair):
        here = pair_of(pair)
        q2, k2, v2 = q[:, here], k[:, here], v[:, here]
        column = lax.broadcasted_iota(jnp.int32, lse.shape, 1)
        parts = []
        logs = lse[...]
        for odd in range(2):
            s = jnp.where(live, dot_nt(q2, of_head(k2, odd)), -1e9)
            top = jnp.max(s, axis=-1, keepdims=True)
            e = jnp.exp(s - top)
            total = jnp.sum(e, axis=-1, keepdims=True)
            parts.append(dot_nn(e.astype(BF16), v2) * (1.0 / total))
            logs = jnp.where(column == 2 * pair + odd, top + jnp.log(total), logs)
        lse[...] = logs
        att[:, here] = jnp.where(odd_lanes(parts[0].shape), parts[1], parts[0]).astype(BF16)

    sent += [move(att, outs[3]), move(lse, outs[4])]
    acc[...] = dot_nt(att[...], w[:, at_o])

    @pl.loop(0, seq // ROWS)
    def _(t):
        rows = pl.ds(pl.multiple_of(t * ROWS, ROWS), ROWS)
        n, r = normalize(x[rows, :].astype(F32) + acc[rows, :] + vec[2:3, :])
        normal[rows, :] = n
        rscale[rows, :] = r
        low[rows, :] = (n * vec[3:4, :] + vec[4:5, :]).astype(BF16)

    sent += [move(s, o) for s, o in zip((normal, rscale, low), outs[5:])]
    wait(sent)


def middle_kernel(load, store, scalars, low_in, normal_in, cot_in, vec, up_bias, *refs):
    first, second, outs, (acc, sums, unit_sums), scratch = refs
    out_out, ghid_out, *grad_outs = outs
    move = Mover(scratch[-1])
    low, normal, cot, act, slope, n2, r2, out, gffn, w_up, w_down, grads = scratch[:-1]
    early = [move(low_in, low)] + load[0](move, scalars, first, w_up)
    late = load[1](move, scalars, second, w_down) + [move(normal_in, normal), move(cot_in, cot)]
    up, down = flat(w_up), flat(w_down)
    seq, features = low.shape
    tiles = up.shape[1] // TILE
    cut = 1 + (len(early) // 2 if len(early) > 2 else 1)
    for n, copies in enumerate((early[:cut], early[cut:])):
        wait(copies)

        @pl.loop(0, tiles // 2)
        def _(t):
            at = (scalars[AT_Y] ^ n) * (tiles // 2) + t
            here = pl.ds(pl.multiple_of(at * TILE, TILE), TILE)
            h = dot_nn(low[...], up[:, here]) + up_bias[0:1, here]
            phi = 0.5 + 0.5 * lax.erf(h * SQRT_HALF)
            act[:, here] = (h * phi).astype(BF16)
            slope[:, here] = (phi + h * jnp.exp(-0.5 * h * h) * INV_ROOT_TWO_PI).astype(BF16)

    wait(late)
    acc[...] = dot_nt(act[...], down[...])
    groups, parts, piece, _ = out.shape
    block = seq // parts
    for part in range(parts):
        rows = pl.ds(part * block, block)
        normed = normal[rows, :] * vec[0:1, :] + vec[1:2, :]
        n, r = normalize(normed + acc[rows, :] + vec[2:3, :])
        n2[rows, :] = n
        r2[rows, :] = r
        at = part * block + lax.broadcasted_iota(jnp.int32, (block, 1), 0)
        final = (n * vec[3:4, :] + vec[4:5, :]) * (at < scalars[LEN]).astype(F32)
        out[:, part] = final.astype(BF16).reshape(groups, piece, features)
    sent = [move(out, out_out)]
    total = [jnp.zeros((1, features), F32)] * 3
    for part in range(parts):
        rows = pl.ds(part * block, block)
        at = part * block + lax.broadcasted_iota(jnp.int32, (block, 1), 0)
        e = cot[:, part].reshape(block, features).astype(F32) * (at < scalars[LEN]).astype(F32)
        n = n2[rows, :]
        grad = norm_backward(e, n, r2[rows, :], vec[3:4, :])
        g = grad.astype(BF16)
        acc[rows, :] = grad
        gffn[rows, :] = g
        more = [column_sum(g.astype(F32)), column_sum(e * n), column_sum(e)]
        total = [a + b for a, b in zip(total, more)]
    sums[...] = jnp.concatenate(total, axis=0)

    for n in range(2):

        @pl.loop(n * tiles // 2, (n + 1) * tiles // 2)
        def _(t):
            here = pl.ds(pl.multiple_of(t * TILE, TILE), TILE)
            store(scalars, grads, 1, t, dot_tn(gffn[...], act[:, here]).astype(BF16))
            g = (dot_nn(gffn[...], down[:, here]) * slope[:, here].astype(F32)).astype(BF16)
            slope[:, here] = g
            unit_sums[0:1, here] = column_sum(g.astype(F32))
            store(scalars, grads, 0, t, dot_tn(low[...], g).astype(BF16))

        done = pl.ds(n * (tiles // 2) * TILE, tiles // 2 * TILE)
        sent.append(move(slope.at[:, done], ghid_out.at[:, done]))
        if len(grad_outs) == 2:
            far = n ^ scalars[AT_Y]
            for c, o in enumerate(grad_outs):
                sent += [move(grads.at[c, 0, :, far], o.at[0, :, far]), move(grads.at[c, 1, far], o.at[1, far])]
    if len(grad_outs) == 1:
        sent.append(move(grads.at[0], grad_outs[0]))
    wait(sent)


def normed_kernel(load, load_out, scalars, ghid_in, second, normal_in, rscale_in, gain, *refs):
    weights, head_weights, _, (first, gattn, gatt, sums), scratch = refs
    move = Mover(scratch[-1])
    ghid, normal, rscale, acc, w_up, w_out = scratch[:-1]
    early = [move(ghid_in, ghid)] + load(move, scalars, weights, w_up)
    late = [move(s, d) for s, d in ((normal_in, normal), (rscale_in, rscale))]
    last = load_out(move, scalars, head_weights, w_out)
    seq, features = second.shape
    wait(early)
    acc[...] = dot_nt(ghid[...], flat(w_up)[...])
    wait(late)
    sums[...] = jnp.zeros_like(sums)

    @pl.loop(0, seq // ROWS)
    def _(t):
        rows = pl.ds(pl.multiple_of(t * ROWS, ROWS), ROWS)
        n = normal[rows, :]
        e = acc[rows, :] + second[rows, :]
        grad = norm_backward(e, n, rscale[rows, :], gain[...])
        g = grad.astype(BF16)
        first[rows, :] = grad
        gattn[rows, :] = g
        more = [column_sum(g.astype(F32)), column_sum(e * n), column_sum(e)]
        sums[...] += jnp.concatenate(more, axis=0)

    wait(last)
    gatt[...] = dot_nn(gattn[...], flat(w_out)[...]).astype(BF16)


def last_kernel(load, store, scalars, gatt, gattn, first, *refs):
    ins, (tokens,), (other,), first_pieces, second_pieces, outs, (sums,), scratch = refs
    own_out, other_out, *grad_outs = outs
    move = Mover(scratch[-1])
    q, k, v, att, lse, x, gq, gk, gv, rows_grad, w5, grads = scratch[:-1]
    early = [move(s, d) for s, d in zip(ins, (q, k, v, att, lse))]
    late = load_tokens(move, scalars, tokens, other, x)
    later = load[0](move, scalars, first_pieces, w5) + load[1](move, scalars, second_pieces, w5)
    wait(early)
    seq, features = q.shape
    scale = HEAD**-0.5
    live = lax.broadcasted_iota(jnp.int32, (1, seq), 1) < scalars[LEN]

    @pl.loop(0, features // PAIR)
    def _(pair):
        here = pair_of(pair)
        q2, k2, v2, do2 = q[:, here], k[:, here], v[:, here], gatt[:, here]
        both = do2.astype(F32) * att[:, here].astype(F32)
        column = lax.broadcasted_iota(jnp.int32, lse.shape, 1)
        logs = lse[...]
        q_turned, do_turned = q2.T, do2.T
        for_q, for_k, for_v = [], [], []
        for odd in range(2):
            log = jnp.sum(jnp.where(column == 2 * pair + odd, logs, 0.0), axis=-1, keepdims=True)
            inner = jnp.sum(of_head(both, odd), axis=-1, keepdims=True)
            s = jnp.where(live, dot_nt(q2, of_head(k2, odd)), -1e9)
            p = jnp.exp(s - log)
            gs = (p * (dot_nt(do2, of_head(v2, odd)) - inner)).astype(BF16)
            for_q.append(dot_nn(gs, k2))
            head = slice(odd * HEAD, (odd + 1) * HEAD)
            for_k.append(dot_nn(q_turned[head], gs))
            for_v.append(dot_nn(do_turned[head], p.astype(BF16)))
        g = (jnp.where(odd_lanes(for_q[0].shape), for_q[1], for_q[0]) * scale).astype(BF16)
        gq[:, here] = g
        sums[0:1, here] = column_sum(g.astype(F32))
        gk[:, here] = jnp.concatenate(for_k, axis=0).astype(BF16).T
        g = jnp.concatenate(for_v, axis=0).astype(BF16).T
        gv[:, here] = g
        sums[1:2, here] = column_sum(g.astype(F32))

    wait(late)
    store(scalars, grads, 0, dot_tn(x[...], gq[...]).astype(BF16))
    store(scalars, grads, 1, dot_tn(x[...], gk[...]).astype(BF16))
    store(scalars, grads, 2, dot_tn(x[...], gv[...]).astype(BF16))
    store(scalars, grads, 3, dot_tn(gattn[...], att[...]).astype(BF16))
    sent = [move(grads.at[n], o) for n, o in enumerate(grad_outs)]
    wait(later)
    w = flat(w5)
    total = first[...]
    for n, g in enumerate((gq, gk, gv)):
        total = total + dot_nt(g[...], w[:, pl.ds(n * features, features)])
    rows_grad[...] = total.astype(BF16)
    half = own_out.shape[0]
    for at, out in ((scalars[AT_Y], own_out), (1 - scalars[AT_Y], other_out)):
        sent.append(move(rows_grad.at[pl.ds(pl.multiple_of(at * half, half), half)], out))
    wait(sent)


def blocks(scalars, rows):
    for at_z in range(4):
        for at_x in range(2):
            for at_c in range(2):
                start = ((at_z * 2 + at_x) * 2 + at_c) * rows
                yield start, at_c ^ scalars[AT_C], at_x ^ scalars[AT_X], at_z ^ scalars[AT_Z]


def store_units(scalars, out, number, t, value):
    rows, width = out.shape[-2:]
    tiles = width // TILE
    col = pl.multiple_of((t % tiles) * TILE, TILE)
    far_y = (t // tiles) ^ scalars[AT_Y]
    for start, far_c, far_x, far_z in blocks(scalars, rows):
        one, two = (far_y, far_x) if number else (far_x, far_y)
        out[far_c, number, one, two, far_z, :, pl.ds(col, TILE)] = value[start : start + rows]


def store_heads(scalars, out, number, value):
    rows, width = out.shape[-2:]
    cols = width // 4
    col = number * cols
    for start, far_c, far_x, far_z in blocks(scalars, rows):
        for at_y in range(2):
            far = far_x * 2 + (at_y ^ scalars[AT_Y])
            piece = value[start : start + rows, at_y * cols : (at_y + 1) * cols]
            out[far_c, far, far_z, :, col : col + cols] = piece


def store_units_whole(scalars, out, number, t, value):
    out[0, number, :, pl.ds(pl.multiple_of(t * TILE, TILE), TILE)] = value


def store_heads_whole(scalars, out, number, value):
    cols = value.shape[1]
    out[0, :, number * cols : (number + 1) * cols] = value


def pick_kernel(scatter, order, src, dst):
    @pl.loop(0, dst.shape[0])
    def _(t):
        if scatter:
            dst[order[t]] = src[t]
        else:
            dst[t] = src[order[t]]


def pick(pieces, order, scatter):
    return pl.pallas_call(
        functools.partial(pick_kernel, scatter),
        out_shape=jax.ShapeDtypeStruct(pieces.shape, pieces.dtype),
        in_specs=[SMEM, VMEM],
        out_specs=VMEM,
        compiler_params=params(4),
        cost_estimate=cost(1),
        name="pick",
    )(order, pieces)


def in_hbm(value):
    return pltpu.with_memory_space_constraint(value, pltpu.HBM)


def in_vmem(value):
    if value.size < 1 << 16:
        return value
    return pltpu.with_memory_space_constraint(value, pltpu.VMEM)


def stays_near(shape):
    return shape if shape.size < 1 << 16 else pltpu.VMEM(shape.shape, shape.dtype)


def run(kernel, name, us, mib, scalars, ins, lists, outs, sums, scratch, sems):
    arrays = [in_vmem(a) if near else in_hbm(a) for a, near in ins] + [in_hbm(a) for some in lists for a in some]
    specs = [VMEM if near else HBM for _, near in ins] + [HBM for some in lists for _ in some]
    groups = [len(some) for some in lists]

    def body(scalars, *refs):
        refs = list(refs)

        def take(n):
            got, refs[:] = refs[:n], refs[n:]
            return got

        singles = take(len(ins))
        grouped = [take(n) for n in groups]
        grouped.append(take(len(outs)))
        if sums:
            grouped.append(take(len(sums)))
        kernel(scalars, *singles, *grouped, refs)

    def buffer(shape):
        return pltpu.VMEM(shape.shape, shape.dtype)

    return pl.pallas_call(
        body,
        out_shape=(*(pltpu.HBM(o.shape, o.dtype) for o in outs), *(stays_near(o) for o in sums)),
        in_specs=[SMEM] + specs,
        out_specs=(HBM,) * len(outs) + (VMEM,) * len(sums),
        scratch_shapes=[*map(buffer, scratch), pltpu.SemaphoreType.DMA((sems,))],
        compiler_params=params(mib),
        cost_estimate=cost(us),
        name=name,
    )(scalars, *arrays)


def add_up(values):
    total = values[0].astype(F32)
    for v in values[1:]:
        total = total + v.astype(F32)
    return total


def pairs(values):
    return (values[0] + values[1]) + (values[2] + values[3])


def split_wide(value):
    high = value.astype(BF16)
    low = (value - high.astype(F32)).astype(BF16)
    both = jnp.concatenate([high, low])
    return jnp.pad(both, ((0, -both.shape[0] % 16), (0, 0)))


def join_wide(rows, count):
    return rows[:count].astype(F32) + rows[count : 2 * count].astype(F32)


class Scatter:
    def __init__(self, keep, send, extra):
        self.keep, self.send, self.extra = keep, send, extra
        self.shape = keep.shape

    def core(self):
        self.got = exchange(self.send, C_BIT), exchange(self.extra, C_BIT)

    def _ready(self, terms):
        self.low = split_wide(self.extra)
        width = self.shape[-1]
        self.sent = [
            jnp.concatenate([add_up([t[m] for t in terms]).astype(BF16).reshape(-1, width), self.low])
            for m in (1, 2, 3)
        ]
        self.terms = [t[0] for t in terms]

    def _go(self, masks):
        self.got = [exchange(s, mask) for s, mask in zip(self.sent, masks)]

    def _came(self):
        rows = self.terms[0].size // self.shape[-1]
        count = self.extra.shape[0]
        self.extra = pairs([join_wide(r, count) for r in (self.low, *(g[rows:] for g in self.got))])
        return [g[:rows].reshape(self.terms[0].shape) for g in self.got]

    def ready_sides(self):
        near, extra = self.got
        self.extra = self.extra + extra
        self._ready([self.keep, near])

    def sides(self):
        self.got = [exchange(self.sent[0], Y_BIT), exchange(self.sent[1], X_BIT)]

    def corner(self):
        self.got.append(exchange(self.sent[2], X_BIT + Y_BIT))

    def along_z(self):
        self._ready(self.terms + self._came())
        self._go((Z_BIT, 2 * Z_BIT, 3 * Z_BIT))

    def total(self):
        return add_up(self.terms + self._came())


def combine_kernel(jobs, tails, *refs):
    refs = list(refs)

    def take(n):
        got, refs[:] = refs[:n], refs[n:]
        return got

    arrays = take(1 + max(n for job in jobs for part in job for n, _ in part))
    rows_in = take(2 if tails else 0)
    outs = take(len(jobs))
    rows_out = take(1 if tails else 0)
    move = Mover(refs.pop())
    into = [take(len(job)) for job in jobs]
    copies = [
        [move(arrays[n].at[at], ref.at[k]) for part, ref in zip(job, some) for k, (n, at) in enumerate(part)]
        for job, some in zip(jobs, into)
    ]
    if tails:
        total = rows_in[0][...] + rows_in[1][...]
        rows_out[0][...] = total
        below = split_wide(total)
    sent = []
    for number, (job, some, made) in enumerate(zip(jobs, into, refs)):
        wait(copies[number])
        at = 0
        for ref in some:
            terms, blocks, high, _ = ref.shape
            for b in range(blocks):
                total = ref[0, b].astype(F32)
                for k in range(1, terms):
                    total = total + ref[k, b].astype(F32)
                made[at : at + high] = total.astype(BF16)
                at += high
        if number in tails:
            made[at:] = below
        sent.append(move(made, outs[number]))
    wait(sent)


def combine(name, us, arrays, jobs, shape, tails=(), rows=()):
    blocks, high, width = shape
    outs = [
        jax.ShapeDtypeStruct((len(job) * blocks * high + (16 if n in tails else 0), width), BF16)
        for n, job in enumerate(jobs)
    ]
    scratch = [pltpu.VMEM((len(part), *shape), BF16) for job in jobs for part in job]
    scratch += [pltpu.VMEM(out.shape, BF16) for out in outs]
    copies = sum(len(part) for job in jobs for part in job) + len(jobs)
    return pl.pallas_call(
        functools.partial(combine_kernel, jobs, tails),
        out_shape=[pltpu.HBM(o.shape, o.dtype) for o in outs]
        + [jax.ShapeDtypeStruct(r.shape, r.dtype) for r in rows[:1]],
        in_specs=[HBM] * len(arrays) + [VMEM] * len(rows),
        out_specs=[HBM] * len(outs) + [VMEM] * len(rows[:1]),
        scratch_shapes=[*scratch, pltpu.SemaphoreType.DMA((copies,))],
        compiler_params=params(12),
        cost_estimate=cost(us),
        name=name,
    )(*map(in_hbm, arrays), *rows)


class ScatterTwo:
    def __init__(self, keep, send):
        self.keep, self.send = keep, send

    def core(self):
        self.got = exchange(self.send, C_BIT)

    def first_side(self):
        rows, width = self.send.shape[-2:]
        keep, near = (a.reshape(2, 2, 8, rows, width) for a in (self.keep, self.got))
        sent = combine("first_side", 3, [keep, near], [[[(n, (h, 1)) for n in range(2)]] for h in range(2)], (8, rows, width))
        self.terms = [[self.keep[h, 0], self.got[h, 0]] for h in range(2)]
        self.got = [exchange(s, m).reshape(2, 4, rows, width) for s, m in zip(sent, (X_BIT, Y_BIT))]

    def side(self, masks):
        got = []
        for n, mask in enumerate(masks):
            terms = self.terms[n] + [self.got[n]]
            got.append(exchange(add_up([t[1] for t in terms]).astype(BF16), mask))
            self.terms[n][:] = [t[0] for t in terms]
        self.got = got

    def along_z(self):
        terms = [self.terms[n] + [self.got[n]] for n in range(2)]
        self.got = []
        for m in (1, 2, 3):
            both = jnp.stack([add_up([t[m] for t in terms[n]]).astype(BF16) for n in range(2)])
            self.got.append(exchange(both, m * Z_BIT))
        self.terms = [[t[0] for t in terms[n]] for n in range(2)]

    def total(self):
        return [add_up(self.terms[n] + [g[n] for g in self.got]) for n in range(2)]


def scatter_whole(grad, rows, cols):
    size = lax.axis_size("tensor")
    parts = grad.reshape(-1, rows, size, cols).transpose(0, 2, 1, 3).reshape(-1, cols)
    return lax.psum_scatter(parts, BOTH, scatter_dimension=0, tiled=True).astype(F32)


def gather_whole(shard):
    size = lax.axis_size("tensor")
    rows, cols = shard.shape
    got = lax.all_gather(shard, BOTH, axis=0, tiled=False).reshape(-1, size, rows, cols)
    return got.transpose(0, 2, 1, 3).reshape(1, 1, 1, -1, size * cols)


def deal_start(block):
    micro, half, features = block.shape
    dp = lax.axis_size("dp")
    piece = half // dp
    pieces = block.reshape(micro, dp, piece, features).transpose(1, 0, 2, 3)
    pieces = pieces.reshape(dp, micro * piece, features)
    return lax.all_to_all(pieces, "dp", split_axis=0, concat_axis=0, tiled=True)


def deal_pick(spread, order, micro):
    dp, tall, features = spread.shape
    return pick(spread.reshape(dp * micro, tall // micro, features), order, True)


def deal_finish(chosen):
    got = lax.all_to_all(chosen, BOTH, split_axis=0, concat_axis=0, tiled=True)
    return got.reshape(lax.axis_size("dp"), lax.axis_size("tensor"), *chosen.shape[1:])


def collect_start(pieces):
    dp, size, piece, features = pieces.shape
    pieces = pieces.reshape(dp * size, piece, features)
    return lax.all_to_all(pieces, BOTH, split_axis=0, concat_axis=0, tiled=True)


def collect_pick(got, order):
    return pick(got, order, False)


def collect_start_back(chosen, micro):
    count, piece, features = chosen.shape
    chosen = chosen.reshape(count // micro, micro * piece, features)
    return lax.all_to_all(chosen, "dp", split_axis=0, concat_axis=0, tiled=True)


def collect_end(back, micro):
    dp, tall, features = back.shape
    back = back.reshape(dp, micro, tall // micro, features).transpose(1, 0, 2, 3)
    return back.reshape(micro, -1, features)


def on_device(
    tokens, cotangent, lengths, slot_order,
    query_weight, key_weight, value_weight, out_weight, up_weight, down_weight,
    query_bias, value_bias, out_bias, up_bias, down_bias,
    first_gain, first_offset, second_gain, second_offset,
):
    micro, half, features = tokens.shape
    dp, size = lax.axis_size("dp"), lax.axis_size("tensor")
    assert micro == size == 2
    dp_pos, at_y = lax.axis_index("dp"), lax.axis_index("tensor")
    rows, cols = query_weight.shape
    unit_cols = up_weight.shape[1]
    units = unit_cols * size
    seq = half * size
    at_c, at_x, at_z = dp_pos & 1, (dp_pos >> 1) & 1, dp_pos >> 2
    scalars = jnp.stack([lengths[dp_pos * size + at_y], at_z, at_x, at_c, at_y]).astype(jnp.int32)

    other_half = exchange(lax.dynamic_index_in_dim(tokens, 1 - at_y, 0, keepdims=False), Y_BIT)
    biases = jnp.concatenate([query_bias, value_bias, up_bias]).reshape(-1, cols)
    other_biases = exchange(biases, Y_BIT)

    def act(shape, dtype=BF16):
        return jax.ShapeDtypeStruct(shape, dtype)

    def merged(shapes):
        return act((len(shapes), *shapes[0].shape))

    split = dp == 16 and rows % 16 == 0
    if split:
        dims = (4, 2, 2, rows)
        places = (at_z, at_x, at_c, at_y)
        heads = Gather(
            jnp.concatenate([query_weight, key_weight], axis=1),
            jnp.concatenate([value_weight, out_weight], axis=1), places,
        )
        wide = Gather(up_weight, down_weight, places)
        heads.along_z()
        wide.along_z()
        heads.got, other_half, other_biases = tie(heads.got, other_half, other_biases)
        heads.first_side()
        heads.got, wide.got[:2] = tie(heads.got, wide.got[:2])
        heads.second_side()
        heads.got, wide.got, cotangent = tie(heads.got, wide.got, cotangent)
        heads.core()
        wide.first_side()
        spread = deal_start(cotangent)
        heads_a, heads_b = heads.pieces()
        heads_a, heads_b, wide.got = tie(heads_a, heads_b, wide.got)
        wide.second_side()
        chosen = deal_pick(spread, slot_order, micro)
        heads_a, heads_b, chosen = tie(heads_a, heads_b, chosen)
        cot = deal_finish(chosen)
        unit_spans = [(0, unit_cols, lambda y: y * unit_cols)]
        head_spans = [
            [(m * cols, cols, lambda y, n=2 * h + m: n * features + y * cols) for m in range(2)] for h in range(2)
        ]
        out_spans = [(cols, cols, lambda y: y * cols)]
        load_units = [functools.partial(load_pieces, second=h, spans=unit_spans) for h in range(2)]
        load_heads = [functools.partial(load_pieces, second=h, spans=head_spans[h]) for h in range(2)]
        load_out = functools.partial(load_pieces, second=1, spans=out_spans)
        put_units, put_heads = store_units, store_heads
        unit_grads = [act((2, 2, 2, 4, rows, unit_cols))] * 2
        head_grads = [act((4, 4, rows, 4 * cols))] * 2
    else:
        dims = (1, 1, 1, features)
        heads_a, heads_b = (
            [jnp.concatenate([gather_whole(w) for w in pair], axis=-1)]
            for pair in ((query_weight, key_weight), (value_weight, out_weight))
        )
        up_in, down_in = [gather_whole(up_weight)], [gather_whole(down_weight)]
        load_units = [functools.partial(load_whole, second=0, spans=[(0, units, 0)])] * 2
        load_heads = [
            functools.partial(load_whole, second=0, spans=[(0, 2 * features, h * 2 * features)]) for h in range(2)
        ]
        load_out = functools.partial(load_whole, second=0, spans=[(features, features, 0)])
        cot = deal_finish(deal_pick(deal_start(cotangent), slot_order, micro))
        put_units, put_heads = store_units_whole, store_heads_whole
        unit_grads = [act((2, features, units))]
        head_grads = [act((features, 4 * features))]

    biases = in_order(at_y, biases, other_biases, 1)
    full_query, full_value = biases[0].reshape(-1), biases[1].reshape(-1)
    full_up = biases[2:].transpose(1, 0, 2).reshape(1, units)

    low_rows, tall, column = act((seq, features)), act((seq, features), F32), act((seq, 1), F32)
    logs, low_units = act((seq, 128), F32), act((seq, units))
    head_vec = jnp.stack([full_query, full_value, out_bias, first_gain, first_offset])
    head_weights, unit_weights = act((*dims, 4 * features)), act((*dims, units))

    q, k, v, att, lse, n1, r1, low = run(
        functools.partial(attend_kernel, load_heads), "attend", 15, 24, scalars,
        [(tokens, False), (other_half, False), (head_vec, True)], [heads_a, heads_b],
        [low_rows] * 4 + [logs, tall, column, low_rows], [],
        [low_rows] * 5 + [logs, tall, column, low_rows, tall, head_weights], 48,
    )
    if split:
        low, wide.got, wide.near = tie(low, wide.got, wide.near)
        wide.core()
        up_in, down_in = wide.pieces()
    else:
        cot = cot.transpose(1, 0, 2, 3).reshape(1, size, half, features)

    middle_vec = jnp.stack([first_gain, first_offset, down_bias, second_gain, second_offset])
    dealt = act((dp, size, half // dp, features) if split else (1, size, half, features))
    out, ghid, *wide_grad, second, down_sums, unit_sums = run(
        functools.partial(middle_kernel, load_units, put_units), "middle", 24, 44, scalars,
        [(low, False), (n1, False), (cot, False), (middle_vec, True), (full_up, True)], [up_in, down_in],
        [dealt, low_units, *unit_grads], [tall, act((3, features), F32), act((1, units), F32)],
        [
            low_rows, tall, dealt, low_units, low_units, tall, column, dealt, low_rows,
            unit_weights, unit_weights, merged(unit_grads),
        ], 44,
    )
    if split:
        wide_sum = ScatterTwo(*wide_grad)
        wide_sum.core()
    else:
        out = out.reshape(size, dp, half // dp, features).transpose(1, 0, 2, 3)
    out = collect_start(out)

    if split:
        ghid, second, wide_sum.got = tie(ghid, second, wide_sum.got)
        wide_sum.first_side()
    first, gattn, gatt, up_sums = run(
        functools.partial(normed_kernel, load_units[0], load_out), "normed", 8, 20, scalars,
        [(ghid, False), (second, True), (n1, False), (r1, False), (first_gain[None], True)], [up_in, heads_b],
        [], [tall, low_rows, low_rows, act((3, features), F32)],
        [low_units, tall, column, tall, unit_weights, act((*dims, features))], 40,
    )
    own_grad, other_grad, *head_grad, head_sums = run(
        functools.partial(last_kernel, load_heads, put_heads), "last", 20, 28, scalars,
        [(gatt, True), (gattn, True), (first, True)], [[q, k, v, att, lse], [tokens], [other_half], heads_a, heads_b],
        [act((half, features)), act((half, features)), *head_grads], [act((2, features), F32)],
        [low_rows] * 4 + [logs] + [low_rows] * 5 + [head_weights, merged(head_grads)], 60,
    )
    sums = jnp.concatenate([down_sums, up_sums, head_sums, unit_sums.reshape(-1, features)])
    if split:
        head_grad, other_grad, sums, wide_sum.got, out = tie(head_grad, other_grad, sums, wide_sum.got, out)
        head_sum = Scatter(*head_grad, sums.reshape(-1, unit_cols))
        head_sum.core()
        wide_sum.side((Y_BIT, X_BIT))
        layer_out = collect_start_back(collect_pick(out, slot_order), micro)
        head_sum.ready_sides()
        head_sum.sent, head_sum.low, wide_sum.got = tie(head_sum.sent, head_sum.low, wide_sum.got)
        head_sum.sides()
        wide_sum.along_z()
        head_sum.sent[2], wide_sum.got[0] = tie(head_sum.sent[2], wide_sum.got[0])
        head_sum.corner()
        head_sum.got, wide_sum.got, layer_out, other_grad = tie(
            head_sum.got, wide_sum.got, layer_out, other_grad
        )
        other_grad = exchange(other_grad, Y_BIT)
        head_sum.along_z()
        layer_out = collect_end(layer_out, micro)
        total = head_sum.total()
        grads = [total[:, n * cols : (n + 1) * cols] for n in range(4)] + wide_sum.total()
        sums = head_sum.extra.reshape(-1, features)
    else:
        layer_out = collect_end(collect_start_back(collect_pick(out, slot_order), micro), micro)
        other_grad = exchange(other_grad, Y_BIT)
        cut = [head_grad[0][:, n * features : (n + 1) * features] for n in range(4)]
        grads = [scatter_whole(g, rows, cols) for g in cut]
        grads += [scatter_whole(wide_grad[0][n], rows, unit_cols) for n in range(2)]
        sums = lax.psum(sums, BOTH)
    input_grad = in_order(at_y, own_grad, other_grad)

    def own(vec, width):
        return lax.dynamic_slice_in_dim(vec, at_y * width, width)

    return (
        layer_out, input_grad, *grads,
        own(sums[6], cols), own(sums[7], cols), sums[3], own(sums[8:].reshape(-1), unit_cols), sums[0],
        sums[4], sums[5], sums[1], sums[2],
    )


def solution(mesh):
    rows = P("dp", "tensor", None)
    weight = P("dp", "tensor")
    cut = P("tensor")
    whole = P()
    return jax.shard_map(
        on_device,
        mesh=mesh,
        in_specs=(rows, rows, whole, whole, *(weight,) * 6, cut, cut, whole, cut, *(whole,) * 5),
        out_specs=(rows, rows, *(weight,) * 6, cut, cut, whole, cut, *(whole,) * 5),
        check_vma=False,
    )
```

profile of v0, /device:TPU:0, one launch (start us, length us, event | category | flops | bytes accessed | tf_op | source)
XLA Modules:
  0.0 278.1 jit_solution(4407779065031945245)
XLA Ops:
  10.6 3.6 %collective-permute-done.4 = f32[6,384]{1,0:T(8,128)S(1)} collective-permute-done((f32[6,384]{1,0:T(8,128)S(1)}, f32[6,384]{1,0:T(8,128)S(1)}, u32[]{:S(2)}, u32[]{:S(2)}) %collective-permute-start.4) | collective-permute-done | bytes 9248 | tf_op jit(solution)/shard_map/ppermute | solution.py:53
  24.2 4.7 %collective-permute-done.7 = bf16[2,48,1536]{2,1,0:T(8,128)(2,1)S(1)} collective-permute-done((bf16[2,48,1536]{2,1,0:T(8,128)(2,1)S(1)}, bf16[2,48,1536]{2,1,0:T(8,128)(2,1)S(1)}, u32[]{:S(2)}, u32[]{:S(2)}) %collective-permute-start.7) | collective-permute-done | bytes 294944 | tf_op jit(solution)/shard_map/ppermute | solution.py:53
  28.9 6.5 %collective-permute-done.8 = bf16[2,48,1536]{2,1,0:T(8,128)(2,1)S(1)} collective-permute-done((bf16[2,48,1536]{2,1,0:T(8,128)(2,1)S(1)}, bf16[2,48,1536]{2,1,0:T(8,128)(2,1)S(1)}, u32[]{:S(2)}, u32[]{:S(2)}) %collective-permute-start.8) | collective-permute-done | bytes 294944 | tf_op jit(solution)/shard_map/ppermute | solution.py:53
  42.1 5.8 %collective-permute-done.12 = bf16[2,48,1536]{2,1,0:T(8,128)(2,1)S(1)} collective-permute-done((bf16[2,48,1536]{2,1,0:T(8,128)(2,1)S(1)}, bf16[2,48,1536]{2,1,0:T(8,128)(2,1)S(1)}, u32[]{:S(2)}, u32[]{:S(2)}) %collective-permute-start.12) | collective-permute-done | bytes 294944 | tf_op jit(solution)/shard_map/ppermute | solution.py:53
  57.1 5.0 %all-to-all-start = ((bf16[16,32,768]{2,1,0:T(8,128)(2,1)}), bf16[16,32,768]{2,1,0:T(8,128)(2,1)S(1)}, u32[]{:S(2)}, u32[]{:S(2)}) async-start(bf16[16,32,768]{2,1,0:T(8,128)(2,1)} %bitcast.174), calls=%async_computation | async-start | bytes 1572864 | tf_op jit(solution)/shard_map/all_to_all | solution.py:688
  62.1 4.2 %collective-permute-done.17 = bf16[4,48,1536]{2,1,0:T(8,128)(2,1)} collective-permute-done((bf16[4,48,1536]{2,1,0:T(8,128)(2,1)}, bf16[4,48,1536]{2,1,0:T(8,128)(2,1)}, u32[]{:S(2)}, u32[]{:S(2)}) %collective-permute-start.17) | collective-permute-done | bytes 589856 | tf_op jit(solution)/shard_map/ppermute | solution.py:53
  66.3 6.1 %collective-permute-done.16 = bf16[4,48,1536]{2,1,0:T(8,128)(2,1)} collective-permute-done((bf16[4,48,1536]{2,1,0:T(8,128)(2,1)}, bf16[4,48,1536]{2,1,0:T(8,128)(2,1)}, u32[]{:S(2)}, u32[]{:S(2)}) %collective-permute-start.16) | collective-permute-done | bytes 589856 | tf_op jit(solution)/shard_map/ppermute | solution.py:53
  82.5 5.8 %all-to-all-start.1 = ((bf16[32,16,768]{2,1,0:T(8,128)(2,1)}), bf16[32,16,768]{2,1,0:T(8,128)(2,1)}, u32[]{:S(2)}, u32[]{:S(2)}) async-start(bf16[32,16,768]{2,1,0:T(8,128)(2,1)} %pick.2), calls=%async_computation.1 | async-start | bytes 1572864 | tf_op jit(solution)/shard_map/all_to_all | solution.py:697
  88.5 15.5 %attend.1 = (bf16[512,768]{1,0:T(8,128)(2,1)}, bf16[512,768]{1,0:T(8,128)(2,1)}, bf16[512,768]{1,0:T(8,128)(2,1)}, bf16[512,768]{1,0:T(8,128)(2,1)}, f32[512,128...) custom-call(s32[5]{0:T(128)S(1)} %stack.144.scalars, ...), custom_call_target="tpu_custom_call" | custom-call | flops 300000000 | bytes 900000 | tf_op jit(solution)/shard_map/attend/pallas_call | solution.py:495
  104.0 4.6 %collective-permute-done.19.refs_11_ = bf16[2,4,48,1536]{3,2,1,0:T(8,128)(2,1)} collective-permute-done((bf16[2,4,48,1536]{3,2,1,0:T(8,128)(2,1)}, bf16[2,4,48,1536]{3,2,1,0:T(8,128)(2,1)}, u32[]{:S(2)}, u32[]{:S(2)}) %collective-permute-start.19) | collective-permute-done | bytes 1179680 | tf_op jit(solution)/shard_map/ppermute | solution.py:53
  108.6 4.2 %collective-permute-done.18.refs_7_ = bf16[2,4,48,1536]{3,2,1,0:T(8,128)(2,1)S(1)} collective-permute-done((bf16[2,4,48,1536]{3,2,1,0:T(8,128)(2,1)S(1)}, bf16[2,4,48,1536]{3,2,1,0:T(8,128)(2,1)S(1)}, u32[]{:S(2)}, u32[]{:S(2)}) %collective-permute-start.18) | collective-permute-done | bytes 1179680 | tf_op jit(solution)/shard_map/ppermute | solution.py:53
  117.7 23.3 %middle.1 = (bf16[16,2,16,768]{3,2,1,0:T(8,128)(2,1)}, bf16[512,3072]{1,0:T(8,128)(2,1)}, bf16[2,2,2,4,48,1536]{5,4,3,2,1,0:T(8,128)(2,1)}, bf16[2,2,2,4,48,1536...) custom-call(s32[5]{0:T(128)S(1)} %stack.144.scalars, ...), custom_call_target="tpu_custom_call" | custom-call | flops 480000000 | bytes 1440000 | tf_op jit(solution)/shard_map/middle/pallas_call | solution.py:495
  141.2 6.2 %all-to-all-start.2 = ((bf16[32,16,768]{2,1,0:T(8,128)(2,1)}), bf16[32,16,768]{2,1,0:T(8,128)(2,1)S(1)}, u32[]{:S(2)}, u32[]{:S(2)}) async-start(bf16[32,16,768]{2,1,0:T(8,128)(2,1)} %bitcast.180), calls=%async_computation.2 | async-start | bytes 1572864 | tf_op jit(solution)/shard_map/all_to_all | solution.py:704
  149.3 3.7 %first_side.1 = (bf16[384,1536]{1,0:T(8,128)(2,1)}, bf16[384,1536]{1,0:T(8,128)(2,1)}) custom-call(bf16[2,2,8,48,1536]{4,3,2,1,0:T(8,128)(2,1)} %bitcast.172, bf16[2,2,8,48,1536]{4,3,2,1,0:T(8,128)(2,1)} %bitcast.25.refs_1_), custom_call_target="tpu_custom_call" | custom-call | flops 60000000 | bytes 180000 | tf_op jit(solution)/shard_map/first_side/pallas_call | solution.py:622
  157.9 10.0 %normed.1 = (f32[512,768]{1,0:T(8,128)S(1)}, bf16[512,768]{1,0:T(8,128)(2,1)S(1)}, bf16[512,768]{1,0:T(8,128)(2,1)S(1)}, f32[3,768]{1,0:T(4,128)S(1)}) custom-call(s32[5]{0:T(128)S(1)} %stack.144.scalars, bf16[512,3072]{1,0:T(8,128)(2,1)} %get-tuple-element.152.refs_0_, f32[512,768]{1,0:T(8,128)S(1)} %get-tuple-element.153.refs_1_, ...), custom_call_target="tpu_custom_call" | custom-call | flops 160000000 | bytes 480000 | tf_op jit(solution)/shard_map/normed/pallas_call | solution.py:495
  167.9 19.2 %last.1 = (bf16[256,768]{1,0:T(8,128)(2,1)}, bf16[256,768]{1,0:T(8,128)(2,1)}, bf16[4,4,48,1536]{3,2,1,0:T(8,128)(2,1)}, bf16[4,4,48,1536]{3,2,1,0:T(8,128)(2,1)}, f32[2,768]{1,0:T(2,128)S(1)}) custom-call(s32[5]{0:T(128)S(1)} %stack.144.scalars, bf16[512,768]{1,0:T(8,128)(2,1)S(1)} %get-tuple-element.155.refs_0_, ...), custom_call_target="tpu_custom_call" | custom-call | flops 400000000 | bytes 1200000 | tf_op jit(solution)/shard_map/last/pallas_call | solution.py:495
  193.5 6.1 %all-to-all-start.3 = ((bf16[16,32,768]{2,1,0:T(8,128)(2,1)}), bf16[16,32,768]{2,1,0:T(8,128)(2,1)S(1)}, u32[]{:S(2)}, u32[]{:S(2)}) async-start(bf16[16,32,768]{2,1,0:T(8,128)(2,1)} %bitcast.48), calls=%async_computation.3 | async-start | bytes 1572864 | tf_op jit(solution)/shard_map/all_to_all | solution.py:714
  203.0 3.8 %collective-permute-done.29 = bf16[4,48,1536]{2,1,0:T(8,128)(2,1)} collective-permute-done((bf16[4,48,1536]{2,1,0:T(8,128)(2,1)}, bf16[4,48,1536]{2,1,0:T(8,128)(2,1)}, u32[]{:S(2)}, u32[]{:S(2)}) %collective-permute-start.29) | collective-permute-done | bytes 589856 | tf_op jit(solution)/shard_map/ppermute | solution.py:53
  206.9 5.2 %collective-permute-done.30 = bf16[4,48,1536]{2,1,0:T(8,128)(2,1)} collective-permute-done((bf16[4,48,1536]{2,1,0:T(8,128)(2,1)}, bf16[4,48,1536]{2,1,0:T(8,128)(2,1)}, u32[]{:S(2)}, u32[]{:S(2)}) %collective-permute-start.30) | collective-permute-done | bytes 589856 | tf_op jit(solution)/shard_map/ppermute | solution.py:53
  217.3 5.3 %collective-permute-done.33 = bf16[2,48,1536]{2,1,0:T(8,128)(2,1)S(1)} collective-permute-done((bf16[2,48,1536]{2,1,0:T(8,128)(2,1)S(1)}, bf16[2,48,1536]{2,1,0:T(8,128)(2,1)S(1)}, u32[]{:S(2)}, u32[]{:S(2)}) %collective-permute-start.33) | collective-permute-done | bytes 294944 | tf_op jit(solution)/shard_map/ppermute | solution.py:53
  224.3 3.8 %collective-permute-start.36 = (bf16[2,48,1536]{2,1,0:T(8,128)(2,1)S(1)}, bf16[2,48,1536]{2,1,0:T(8,128)(2,1)}, u32[]{:S(2)}, u32[]{:S(2)}) collective-permute-start(bf16[2,48,1536]{2,1,0:T(8,128)(2,1)S(1)} %pad_maximum_fusion.18), channel_id=1, source_target_pairs={{0,24},{1,25},{2,26},{3,27},{4,28},{5,29},{6,30},{7,31},{8,16},{9,... | collective-permute-start | bytes 884744 | tf_op jit(solution)/shard_map/ppermute | solution.py:53
  228.8 7.4 %collective-permute-done.36 = bf16[2,48,1536]{2,1,0:T(8,128)(2,1)} collective-permute-done((bf16[2,48,1536]{2,1,0:T(8,128)(2,1)S(1)}, bf16[2,48,1536]{2,1,0:T(8,128)(2,1)}, u32[]{:S(2)}, u32[]{:S(2)}) %collective-permute-start.36) | collective-permute-done | bytes 294944 | tf_op jit(solution)/shard_map/ppermute | solution.py:53
  236.2 14.9 %collective-permute-done.35 = bf16[2,48,1536]{2,1,0:T(8,128)(2,1)} collective-permute-done((bf16[2,48,1536]{2,1,0:T(8,128)(2,1)}, bf16[2,48,1536]{2,1,0:T(8,128)(2,1)}, u32[]{:S(2)}, u32[]{:S(2)}) %collective-permute-start.35) | collective-permute-done | bytes 294944 | tf_op jit(solution)/shard_map/ppermute | solution.py:53
  264.1 6.8 %collective-permute-done.39 = bf16[64,1536]{1,0:T(8,128)(2,1)S(1)} collective-permute-done((bf16[64,1536]{1,0:T(8,128)(2,1)S(1)}, bf16[64,1536]{1,0:T(8,128)(2,1)S(1)}, u32[]{:S(2)}, u32[]{:S(2)}) %collective-permute-start.39) | collective-permute-done | bytes 196640 | tf_op jit(solution)/shard_map/ppermute | solution.py:53
  (247 shorter events, 94.7 us)
Async XLA Ops:
  1.8 19.5 %collective-permute-start.3 = (bf16[256,768]{1,0:T(8,128)(2,1)S(1)}, bf16[256,768]{1,0:T(8,128)(2,1)S(1)}, u32[]{:S(2)}, u32[]{:S(2)}) collective-permute-start(bf16[256,768]{1,0:T(8,128)(2,1)S(1)} %dynamic-slice_bitcast_fusion), channel_id=1, source_target_pairs={{0,1},{1,0},{2,3},{3,2},{4,5},{5,4},{6,7},{7,6},{8,9},{9,8},{10,11... | collective-permute-start | bytes 1179656 | tf_op jit(solution)/shard_map/ppermute | solution.py:53
  16.0 19.4 %collective-permute-start.8 = (bf16[2,48,1536]{2,1,0:T(8,128)(2,1)S(1)}, bf16[2,48,1536]{2,1,0:T(8,128)(2,1)S(1)}, u32[]{:S(2)}, u32[]{:S(2)}) collective-permute-start(bf16[2,48,1536]{2,1,0:T(8,128)(2,1)S(1)} %pad_maximum_fusion.15), channel_id=1, source_target_pairs={{0,16},{1,17},{2,18},{3,19},{4,20},{5,21},{6,22},{7,23},{8,24},{9,... | collective-permute-start | bytes 884744 | tf_op jit(solution)/shard_map/ppermute | solution.py:53
  41.6 20.5 %collective-permute-start.9 = (bf16[2,4,48,768]{3,2,1,0:T(8,128)(2,1)}, bf16[2,4,48,768]{3,2,1,0:T(8,128)(2,1)}, u32[]{:S(2)}, u32[]{:S(2)}) collective-permute-start(bf16[2,4,48,768]{3,2,1,0:T(8,128)(2,1)} %pad_maximum_fusion.6.refs_3_.refs_10_), channel_id=1, source_target_pairs={{0,2},{1,3},{2,0},{3,1},{4,6},{5,7},{6,4},{7,5},{8,10},{9,11},{10,... | collective-permute-start | bytes 1769480 | tf_op jit(solution)/shard_map/ppermute | solution.py:53
  54.9 17.5 %collective-permute-start.16 = (bf16[4,48,1536]{2,1,0:T(8,128)(2,1)}, bf16[4,48,1536]{2,1,0:T(8,128)(2,1)}, u32[]{:S(2)}, u32[]{:S(2)}) collective-permute-start(bf16[4,48,1536]{2,1,0:T(8,128)(2,1)} %pad_maximum_fusion.8), channel_id=1, source_target_pairs={{0,4},{1,5},{2,6},{3,7},{4,0},{5,1},{6,2},{7,3},{8,12},{9,13},{10,... | collective-permute-start | bytes 1769480 | tf_op jit(solution)/shard_map/ppermute | solution.py:53
  55.5 16.9 %collective-permute-start.13 = (bf16[2,4,48,768]{3,2,1,0:T(8,128)(2,1)S(1)}, bf16[2,4,48,768]{3,2,1,0:T(8,128)(2,1)}, u32[]{:S(2)}, u32[]{:S(2)}) collective-permute-start(bf16[2,4,48,768]{3,2,1,0:T(8,128)(2,1)S(1)} %collective-permute-done.10.refs_5_.refs_12_), channel_id=1, source_target_pairs={{0,2},{1,3},{2,0},{3,1},{4,6},{5,7},{6,4},{7,5},{8,10},{9,11},{10,... | collective-permute-start | bytes 1769480 | tf_op jit(solution)/shard_map/ppermute | solution.py:53
  55.6 16.9 %collective-permute-start.15 = (bf16[2,4,48,768]{3,2,1,0:T(8,128)(2,1)S(1)}, bf16[2,4,48,768]{3,2,1,0:T(8,128)(2,1)S(1)}, u32[]{:S(2)}, u32[]{:S(2)}) collective-permute-start(bf16[2,4,48,768]{3,2,1,0:T(8,128)(2,1)S(1)} %collective-permute-done.11.refs_9_.refs_11_.refs_16_), channel_id=1, source_target_pairs={{0,2},{1,3},{2,0},{3,1},{4,6},{5,7},{6,4},{7,5},{8,10},{9,11},{10,... | collective-permute-start | bytes 1769480 | tf_op jit(solution)/shard_map/ppermute | solution.py:53
  57.1 23.8 %all-to-all-start = ((bf16[16,32,768]{2,1,0:T(8,128)(2,1)}), bf16[16,32,768]{2,1,0:T(8,128)(2,1)S(1)}, u32[]{:S(2)}, u32[]{:S(2)}) async-start(bf16[16,32,768]{2,1,0:T(8,128)(2,1)} %bitcast.174), calls=%async_computation | async-start | bytes 1572864 | tf_op jit(solution)/shard_map/all_to_all | solution.py:688
  75.2 33.4 %collective-permute-start.19 = (bf16[2,4,48,1536]{3,2,1,0:T(8,128)(2,1)}, bf16[2,4,48,1536]{3,2,1,0:T(8,128)(2,1)}, u32[]{:S(2)}, u32[]{:S(2)}) collective-permute-start(bf16[2,4,48,1536]{3,2,1,0:T(8,128)(2,1)} %pad_maximum_fusion.1.refs_9_), channel_id=1, source_target_pairs={{0,4},{1,5},{2,6},{3,7},{4,0},{5,1},{6,2},{7,3},{8,12},{9,13},{10,... | collective-permute-start | bytes 3538952 | tf_op jit(solution)/shard_map/ppermute | solution.py:53
  75.2 33.4 %collective-permute-start.21 = (bf16[2,4,48,1536]{3,2,1,0:T(8,128)(2,1)}, bf16[2,4,48,1536]{3,2,1,0:T(8,128)(2,1)}, u32[]{:S(2)}, u32[]{:S(2)}) collective-permute-start(bf16[2,4,48,1536]{3,2,1,0:T(8,128)(2,1)} %pad_maximum_fusion.1.refs_9_), channel_id=1, source_target_pairs={{0,2},{1,3},{2,0},{3,1},{4,6},{5,7},{6,4},{7,5},{8,10},{9,11},{10,... | collective-permute-start | bytes 3538952 | tf_op jit(solution)/shard_map/ppermute | solution.py:53
  76.6 36.2 %collective-permute-start.18 = (bf16[2,4,48,1536]{3,2,1,0:T(8,128)(2,1)S(1)}, bf16[2,4,48,1536]{3,2,1,0:T(8,128)(2,1)S(1)}, u32[]{:S(2)}, u32[]{:S(2)}) collective-permute-start(bf16[2,4,48,1536]{3,2,1,0:T(8,128)(2,1)S(1)} %pad_maximum_fusion.refs_5_), channel_id=1, source_target_pairs={{0,1},{1,0},{2,3},{3,2},{4,5},{5,4},{6,7},{7,6},{8,9},{9,8},{10,11... | collective-permute-start | bytes 3538952 | tf_op jit(solution)/shard_map/ppermute | solution.py:53
  78.2 34.6 %collective-permute-start.20 = (bf16[2,4,48,1536]{3,2,1,0:T(8,128)(2,1)S(1)}, bf16[2,4,48,1536]{3,2,1,0:T(8,128)(2,1)}, u32[]{:S(2)}, u32[]{:S(2)}) collective-permute-start(bf16[2,4,48,1536]{3,2,1,0:T(8,128)(2,1)S(1)} %pad_maximum_fusion.refs_5_), channel_id=1, source_target_pairs={{0,2},{1,3},{2,0},{3,1},{4,6},{5,7},{6,4},{7,5},{8,10},{9,11},{10,... | collective-permute-start | bytes 3538952 | tf_op jit(solution)/shard_map/ppermute | solution.py:53
  82.5 35.2 %all-to-all-start.1 = ((bf16[32,16,768]{2,1,0:T(8,128)(2,1)}), bf16[32,16,768]{2,1,0:T(8,128)(2,1)}, u32[]{:S(2)}, u32[]{:S(2)}) async-start(bf16[32,16,768]{2,1,0:T(8,128)(2,1)} %pick.2), calls=%async_computation.1 | async-start | bytes 1572864 | tf_op jit(solution)/shard_map/all_to_all | solution.py:697
  141.2 46.0 %all-to-all-start.2 = ((bf16[32,16,768]{2,1,0:T(8,128)(2,1)}), bf16[32,16,768]{2,1,0:T(8,128)(2,1)S(1)}, u32[]{:S(2)}, u32[]{:S(2)}) async-start(bf16[32,16,768]{2,1,0:T(8,128)(2,1)} %bitcast.180), calls=%async_computation.2 | async-start | bytes 1572864 | tf_op jit(solution)/shard_map/all_to_all | solution.py:704
  153.1 34.1 %collective-permute-start.25 = (bf16[384,1536]{1,0:T(8,128)(2,1)}, bf16[384,1536]{1,0:T(8,128)(2,1)}, u32[]{:S(2)}, u32[]{:S(2)}) collective-permute-start(bf16[384,1536]{1,0:T(8,128)(2,1)} %get-tuple-element.172), channel_id=1, source_target_pairs={{0,4},{1,5},{2,6},{3,7},{4,0},{5,1},{6,2},{7,3},{8,12},{9,13},{10,... | collective-permute-start | bytes 3538952 | tf_op jit(solution)/shard_map/ppermute | solution.py:53
  155.2 32.0 %collective-permute-start.26 = (bf16[384,1536]{1,0:T(8,128)(2,1)}, bf16[384,1536]{1,0:T(8,128)(2,1)}, u32[]{:S(2)}, u32[]{:S(2)}) collective-permute-start(bf16[384,1536]{1,0:T(8,128)(2,1)} %get-tuple-element.173), channel_id=1, source_target_pairs={{0,1},{1,0},{2,3},{3,2},{4,5},{5,4},{6,7},{7,6},{8,9},{9,8},{10,11... | collective-permute-start | bytes 3538952 | tf_op jit(solution)/shard_map/ppermute | solution.py:53
  191.3 15.6 %collective-permute-start.29 = (bf16[4,48,1536]{2,1,0:T(8,128)(2,1)}, bf16[4,48,1536]{2,1,0:T(8,128)(2,1)}, u32[]{:S(2)}, u32[]{:S(2)}) collective-permute-start(bf16[4,48,1536]{2,1,0:T(8,128)(2,1)} %get-tuple-element.216), channel_id=1, source_target_pairs={{0,1},{1,0},{2,3},{3,2},{4,5},{5,4},{6,7},{7,6},{8,9},{9,8},{10,11... | collective-permute-start | bytes 1769480 | tf_op jit(solution)/shard_map/ppermute | solution.py:53
  191.8 20.3 %collective-permute-start.30 = (bf16[4,48,1536]{2,1,0:T(8,128)(2,1)}, bf16[4,48,1536]{2,1,0:T(8,128)(2,1)}, u32[]{:S(2)}, u32[]{:S(2)}) collective-permute-start(bf16[4,48,1536]{2,1,0:T(8,128)(2,1)} %get-tuple-element.215), channel_id=1, source_target_pairs={{0,4},{1,5},{2,6},{3,7},{4,0},{5,1},{6,2},{7,3},{8,12},{9,13},{10,... | collective-permute-start | bytes 1769480 | tf_op jit(solution)/shard_map/ppermute | solution.py:53
  193.5 35.3 %all-to-all-start.3 = ((bf16[16,32,768]{2,1,0:T(8,128)(2,1)}), bf16[16,32,768]{2,1,0:T(8,128)(2,1)S(1)}, u32[]{:S(2)}, u32[]{:S(2)}) async-start(bf16[16,32,768]{2,1,0:T(8,128)(2,1)} %bitcast.48), calls=%async_computation.3 | async-start | bytes 1572864 | tf_op jit(solution)/shard_map/all_to_all | solution.py:714
  215.7 35.5 %collective-permute-start.31 = (bf16[208,1536]{1,0:T(8,128)(2,1)}, bf16[208,1536]{1,0:T(8,128)(2,1)}, u32[]{:S(2)}, u32[]{:S(2)}) collective-permute-start(bf16[208,1536]{1,0:T(8,128)(2,1)} %get-tuple-element.180), channel_id=1, source_target_pairs={{0,1},{1,0},{2,3},{3,2},{4,5},{5,4},{6,7},{7,6},{8,9},{9,8},{10,11... | collective-permute-start | bytes 1916936 | tf_op jit(solution)/shard_map/ppermute | solution.py:53
  217.3 33.9 %collective-permute-start.32 = (bf16[208,1536]{1,0:T(8,128)(2,1)}, bf16[208,1536]{1,0:T(8,128)(2,1)}, u32[]{:S(2)}, u32[]{:S(2)}) collective-permute-start(bf16[208,1536]{1,0:T(8,128)(2,1)} %get-tuple-element.181), channel_id=1, source_target_pairs={{0,4},{1,5},{2,6},{3,7},{4,0},{5,1},{6,2},{7,3},{8,12},{9,13},{10,... | collective-permute-start | bytes 1916936 | tf_op jit(solution)/shard_map/ppermute | solution.py:53
  222.6 28.6 %collective-permute-start.34 = (bf16[208,1536]{1,0:T(8,128)(2,1)}, bf16[208,1536]{1,0:T(8,128)(2,1)}, u32[]{:S(2)}, u32[]{:S(2)}) collective-permute-start(bf16[208,1536]{1,0:T(8,128)(2,1)} %get-tuple-element.185), channel_id=1, source_target_pairs={{0,5},{1,4},{2,7},{3,6},{4,1},{5,0},{6,3},{7,2},{8,13},{9,12},{10,... | collective-permute-start | bytes 1916936 | tf_op jit(solution)/shard_map/ppermute | solution.py:53
  228.8 22.3 %collective-permute-start.35 = (bf16[2,48,1536]{2,1,0:T(8,128)(2,1)}, bf16[2,48,1536]{2,1,0:T(8,128)(2,1)}, u32[]{:S(2)}, u32[]{:S(2)}) collective-permute-start(bf16[2,48,1536]{2,1,0:T(8,128)(2,1)} %pad_maximum_fusion.17), channel_id=1, source_target_pairs={{0,16},{1,17},{2,18},{3,19},{4,20},{5,21},{6,22},{7,23},{8,24},{9,... | collective-permute-start | bytes 884744 | tf_op jit(solution)/shard_map/ppermute | solution.py:53
  254.1 16.8 %collective-permute-start.39 = (bf16[64,1536]{1,0:T(8,128)(2,1)S(1)}, bf16[64,1536]{1,0:T(8,128)(2,1)S(1)}, u32[]{:S(2)}, u32[]{:S(2)}) collective-permute-start(bf16[64,1536]{1,0:T(8,128)(2,1)S(1)} %get-tuple-element.266), channel_id=1, source_target_pairs={{0,16},{1,17},{2,18},{3,19},{4,20},{5,21},{6,22},{7,23},{8,24},{9,... | collective-permute-start | bytes 589832 | tf_op jit(solution)/shard_map/ppermute | solution.py:53
  258.5 18.6 %collective-permute-start.37 = (bf16[256,768]{1,0:T(8,128)(2,1)}, bf16[256,768]{1,0:T(8,128)(2,1)S(1)}, u32[]{:S(2)}, u32[]{:S(2)}) collective-permute-start(bf16[256,768]{1,0:T(8,128)(2,1)} %get-tuple-element.191), channel_id=1, source_target_pairs={{0,1},{1,0},{2,3},{3,2},{4,5},{5,4},{6,7},{7,6},{8,9},{9,8},{10,11... | collective-permute-start | bytes 1179656 | tf_op jit(solution)/shard_map/ppermute | solution.py:53
  (67 other events, 513.4 us)
where the time goes:
time: 279 us; the launch traced here: 278 us
  waiting for transfers between devices  99.1 us (36%)
  Pallas kernels  75.1 us (27%)
  starting transfers between devices  63.5 us (23%)
  other arithmetic  27.7 us (10%)
  local copies, waits for them, and re-layouts  11.1 us (4%)
    ppermute x41, waiting for transfers between devices, exchange(): return lax.ppermute(value, BOTH, [(i, i ^ mask) for i in range(count)])  98 us
    pallas_call x4, Pallas kernels, run(): pl.pallas_call(body, out_shape=(*(pltpu.HBM(o.shape, o.dtype) for o in ou...  68 us
    ppermute x41, starting transfers between devices, exchange(): return lax.ppermute(value, BOTH, [(i, i ^ mask) for i in range(count)])  40.4 us
    all_to_all x1, starting transfers between devices, collect_start(): return lax.all_to_all(pieces, BOTH, split_axis=0, concat_axis=0, tiled=True)  6.19 us
    all_to_all x1, starting transfers between devices, collect_start_back(): return lax.all_to_all(chosen, 'dp', split_axis=0, concat_axis=0, tiled=True)  6.15 us
    another operation x11, other arithmetic, in_order(): return jnp.stack([low, high], axis=axis)  6.12 us
    all_to_all x1, starting transfers between devices, deal_finish(): got = lax.all_to_all(chosen, BOTH, split_axis=0, concat_axis=0, tiled=True)  5.76 us
  transfers between devices with their start and end apart: 45, of which 22 were waited for; matrix products, arithmetic and copies ran while one was open for 11% of the time, Pallas kernels for 19%

commit v1 on v0

--- a/solution.py
+++ b/solution.py
@@ -81,9 +81,8 @@
         self.got = exchange(self.a, X_BIT), exchange(self.b, Y_BIT)
 
     def second_side(self):
-        _, at_x, _, at_y = self.places
-        self.a = in_order(at_x, self.a, self.got[0])
-        self.b = in_order(at_y, self.b, self.got[1])
+        self.a = jnp.stack([self.a, self.got[0]])
+        self.b = jnp.stack([self.b, self.got[1]])
         self.got = exchange(self.a, Y_BIT), exchange(self.b, X_BIT)
         self.near = exchange(self.a, C_BIT), exchange(self.b, C_BIT)
 
@@ -120,9 +119,9 @@
         at_c = scalars[AT_C] ^ other
         for inner in range(2):
             if second:
-                at_x, at_y = scalars[AT_X] ^ far, inner
+                at_x, at_y = scalars[AT_X] ^ far, scalars[AT_Y] ^ inner
             else:
-                at_x, at_y = inner, scalars[AT_Y] ^ far
+                at_x, at_y = scalars[AT_X] ^ inner, scalars[AT_Y] ^ far
             for start, width, to in spans:
                 column = pl.multiple_of(to(at_y), 128)
                 copies.append(
@@ -344,7 +343,11 @@
     own_out, other_out, *grad_outs = outs
     move = Mover(scratch[-1])
     q, k, v, att, lse, x, gq, gk, gv, rows_grad, w5, grads = scratch[:-1]
-    early = [move(s, d) for s, d in zip(ins, (q, k, v, att, lse))]
+    width = q.shape[1] // 2
+    early = [move(ins[4], lse)]
+    halves = []
+    for at in (pl.ds(0, width), pl.ds(width, width)):
+        halves.append([move(s.at[:, at], d.at[:, at]) for s, d in zip(ins, (q, k, v, att))])
     late = load_tokens(move, scalars, tokens, other, x)
     later = load[0](move, scalars, first_pieces, w5) + load[1](move, scalars, second_pieces, w5)
     wait(early)
@@ -352,8 +355,7 @@
     scale = HEAD**-0.5
     live = lax.broadcasted_iota(jnp.int32, (1, seq), 1) < scalars[LEN]
 
-    @pl.loop(0, features // PAIR)
-    def _(pair):
+    def one_pair(pair):
         here = pair_of(pair)
         q2, k2, v2, do2 = q[:, here], k[:, here], v[:, here], gatt[:, here]
         both = do2.astype(F32) * att[:, here].astype(F32)
@@ -379,6 +381,11 @@
         gv[:, here] = g
         sums[1:2, here] = column_sum(g.astype(F32))
 
+    pairs_there = features // PAIR // 2
+    for n, copies in enumerate(halves):
+        wait(copies)
+        pl.loop(n * pairs_there, (n + 1) * pairs_there)(one_pair)
+
     wait(late)
     store(scalars, grads, 0, dot_tn(x[...], gq[...]).astype(BF16))
     store(scalars, grads, 1, dot_tn(x[...], gk[...]).astype(BF16))
@@ -518,12 +525,63 @@
 def split_wide(value):
     high = value.astype(BF16)
     low = (value - high.astype(F32)).astype(BF16)
+    space = ((0, 8 - value.shape[0]), (0, 0))
+    return jnp.concatenate([jnp.pad(high, space), jnp.pad(low, space)])
+
+
+def join_wide(rows, count):
+    return rows[:count].astype(F32) + rows[8 : 8 + count].astype(F32)
+
+
+def pairs(values):
+    return (values[0] + values[1]) + (values[2] + values[3])
+
+
+def split_wide(value):
+    high = value.astype(BF16)
+    low = (value - high.astype(F32)).astype(BF16)
     both = jnp.concatenate([high, low])
     return jnp.pad(both, ((0, -both.shape[0] % 16), (0, 0)))
 
 
 def join_wide(rows, count):
     return rows[:count].astype(F32) + rows[count : 2 * count].astype(F32)
+
+
+def finish_kernel(partial, own, first, second, third, *refs):
+    outs, extra = refs[:-1], refs[-1]
+    rows = partial.shape[0]
+    last = [r[...].astype(F32) for r in (first, second, third)]
+    total = partial[...] + last[0][:rows] + last[1][:rows] + last[2][:rows]
+    cols = outs[0].shape[1]
+    for n, out in enumerate(outs):
+        out[...] = total[:, n * cols : (n + 1) * cols]
+    low = own[...].astype(F32)
+    extra[...] = pairs([r[:8] + r[8:] for r in (low, *(v[rows:] for v in last))])
+
+
+def turn_kernel(keep, near, *refs):
+    got, low = refs[:3], refs[3]
+    sent, partial, next_low = refs[4:7], refs[7], refs[8]
+    a, b, *parts, tails, sems = refs[9:]
+    move = Mover(sems)
+    blocks, rows, _ = a.shape
+    copies = [move(keep.at[0], a), move(near.at[0], b)] + [move(g, p) for g, p in zip(got, parts)]
+    wait(copies)
+    extra = [low[...]] + [p[blocks * rows :] for p in parts]
+    extra = pairs([(lambda v: v[:8] + v[8:])(e.astype(F32)) for e in extra])
+    tails[...] = split_wide(extra)
+    next_low[...] = tails[...]
+    for z in range(blocks):
+        at = slice(z * rows, (z + 1) * rows)
+        total = a[z].astype(F32) + b[z].astype(F32)
+        for p in parts:
+            total = total + p[at].astype(F32)
+        if z == 0:
+            partial[...] = total
+        else:
+            sent[z - 1][:rows] = total.astype(BF16)
+            sent[z - 1][rows:] = tails[...]
 
 
 class Scatter:
@@ -554,6 +612,7 @@
 
     def ready_sides(self):
         near, extra = self.got
+        self.near = near
         self.extra = self.extra + extra
         self._ready([self.keep, near])
 
@@ -564,11 +623,38 @@
         self.got.append(exchange(self.sent[2], X_BIT + Y_BIT))
 
     def along_z(self):
-        self._ready(self.terms + self._came())
-        self._go((Z_BIT, 2 * Z_BIT, 3 * Z_BIT))
-
-    def total(self):
-        return add_up(self.terms + self._came())
+        blocks, rows, width = self.shape[1:]
+        low = jax.ShapeDtypeStruct((16, width), BF16)
+        tall = jax.ShapeDtypeStruct((rows + 16, width), BF16)
+        part = pltpu.VMEM((blocks, rows, width), BF16)
+        *sent, self.partial, self.low = pl.pallas_call(
+            turn_kernel,
+            out_shape=(*(tall,) * 3, jax.ShapeDtypeStruct((rows, width), F32), low),
+            in_specs=[HBM] * 5 + [VMEM],
+            out_specs=(VMEM,) * 5,
+            scratch_shapes=[
+                part, part, *[pltpu.VMEM((blocks * rows + 16, width), BF16)] * 3, pltpu.VMEM((16, width), BF16),
+                pltpu.SemaphoreType.DMA((5,)),
+            ],
+            compiler_params=params(10),
+            cost_estimate=cost(2),
+            name="turn",
+        )(*map(in_hbm, (self.keep, self.near, *self.got)), self.low)
+        self.got = [exchange(s, m * Z_BIT) for s, m in zip(sent, (1, 2, 3))]
+
+    def finish(self, count):
+        rows, width = self.shape[-2:]
+        shapes = [jax.ShapeDtypeStruct((rows, width // count), F32)] * count
+        *grads, extra = pl.pallas_call(
+            finish_kernel,
+            out_shape=(*shapes, jax.ShapeDtypeStruct((8, width), F32)),
+            in_specs=[VMEM] * 5,
+            out_specs=(VMEM,) * (count + 1),
+            compiler_params=params(6),
+            cost_estimate=cost(2),
+            name="finish",
+        )(self.partial, self.low, *self.got)
+        return grads, extra[: self.extra.shape[0]]
 
 
 def combine_kernel(jobs, tails, *refs):
@@ -640,30 +726,38 @@
         self.got = exchange(self.send, C_BIT)
 
     def first_side(self):
-        rows, width = self.send.shape[-2:]
-        keep, near = (a.reshape(2, 2, 8, rows, width) for a in (self.keep, self.got))
-        sent = combine("first_side", 3, [keep, near], [[[(n, (h, 1)) for n in range(2)]] for h in range(2)], (8, rows, width))
-        self.terms = [[self.keep[h, 0], self.got[h, 0]] for h in range(2)]
-        self.got = [exchange(s, m).reshape(2, 4, rows, width) for s, m in zip(sent, (X_BIT, Y_BIT))]
-
-    def side(self, masks):
-        got = []
-        for n, mask in enumerate(masks):
-            terms = self.terms[n] + [self.got[n]]
-            got.append(exchange(add_up([t[1] for t in terms]).astype(BF16), mask))
-            self.terms[n][:] = [t[0] for t in terms]
-        self.got = got
+        self.rows, self.width = self.send.shape[-2:]
+        self.arrays = [a.reshape(2, 2, 8, self.rows, self.width) for a in (self.keep, self.got)]
+        sent = combine(
+            "first_side", 3, self.arrays, [[[(n, (h, 1)) for n in range(2)]] for h in range(2)], (8, self.rows, self.width)
+        )
+        self.got = [exchange(s, m).reshape(8, self.rows, self.width) for s, m in zip(sent, (X_BIT, Y_BIT))]
+
+    def second_side(self):
+        self.arrays += self.got
+        far = pl.ds(4, 4)
+        sent = combine(
+            "second_side", 3, self.arrays,
+            [[[(0, (h, 0, far)), (1, (h, 0, far)), (2 + h, (far,))]] for h in range(2)],
+            (4, self.rows, self.width),
+        )
+        self.got = [exchange(s, m).reshape(4, self.rows, self.width) for s, m in zip(sent, (Y_BIT, X_BIT))]
 
     def along_z(self):
-        terms = [self.terms[n] + [self.got[n]] for n in range(2)]
-        self.got = []
-        for m in (1, 2, 3):
-            both = jnp.stack([add_up([t[m] for t in terms[n]]).astype(BF16) for n in range(2)])
-            self.got.append(exchange(both, m * Z_BIT))
-        self.terms = [[t[0] for t in terms[n]] for n in range(2)]
+        self.arrays += self.got
+        jobs = [
+            [[(0, (h, 0, at)), (1, (h, 0, at)), (2 + h, (at,)), (4 + h, (at,))] for h in range(2)]
+            for at in (pl.ds(m, 1) for m in (1, 2, 3))
+        ]
+        sent = combine("along_z", 3, self.arrays, jobs, (1, self.rows, self.width))
+        self.got = [exchange(s, m * Z_BIT) for s, m in zip(sent, (1, 2, 3))]
 
     def total(self):
-        return [add_up(self.terms[n] + [g[n] for g in self.got]) for n in range(2)]
+        sums = []
+        for h in range(2):
+            terms = [self.arrays[n][h, 0, 0] for n in range(2)] + [self.arrays[n + h][0] for n in (2, 4)]
+            sums.append(add_up(terms + [g[h * self.rows : (h + 1) * self.rows] for g in self.got]))
+        return sums
 
 
 def scatter_whole(grad, rows, cols):
@@ -860,31 +954,29 @@
         head_grad, other_grad, sums, wide_sum.got, out = tie(head_grad, other_grad, sums, wide_sum.got, out)
         head_sum = Scatter(*head_grad, sums.reshape(-1, unit_cols))
         head_sum.core()
-        wide_sum.side((Y_BIT, X_BIT))
+        wide_sum.second_side()
         layer_out = collect_start_back(collect_pick(out, slot_order), micro)
         head_sum.ready_sides()
         head_sum.sent, head_sum.low, wide_sum.got = tie(head_sum.sent, head_sum.low, wide_sum.got)
         head_sum.sides()
         wide_sum.along_z()
-        head_sum.sent[2], wide_sum.got[0] = tie(head_sum.sent[2], wide_sum.got[0])
         head_sum.corner()
         head_sum.got, wide_sum.got, layer_out, other_grad = tie(
             head_sum.got, wide_sum.got, layer_out, other_grad
         )
-        other_grad = exchange(other_grad, Y_BIT)
+        input_grad = in_order(at_y, own_grad, exchange(other_grad, Y_BIT))
         head_sum.along_z()
         layer_out = collect_end(layer_out, micro)
-        total = head_sum.total()
-        grads = [total[:, n * cols : (n + 1) * cols] for n in range(4)] + wide_sum.total()
-        sums = head_sum.extra.reshape(-1, features)
+        grads, sums = head_sum.finish(4)
+        grads += wide_sum.total()
+        sums = sums.reshape(-1, features)
     else:
         layer_out = collect_end(collect_start_back(collect_pick(out, slot_order), micro), micro)
-        other_grad = exchange(other_grad, Y_BIT)
+        input_grad = in_order(at_y, own_grad, exchange(other_grad, Y_BIT))
         cut = [head_grad[0][:, n * features : (n + 1) * features] for n in range(4)]
         grads = [scatter_whole(g, rows, cols) for g in cut]
         grads += [scatter_whole(wide_grad[0][n], rows, unit_cols) for n in range(2)]
         sums = lax.psum(sums, BOTH)
-    input_grad = in_order(at_y, own_grad, other_grad)
 
     def own(vec, width):
         return lax.dynamic_slice_in_dim(vec, at_y * width, width)

time: 279 us -> 270 us (0.968)
  other arithmetic: 27.7 us -> 14.5 us
  waiting for transfers between devices: 99.1 us -> 89.8 us
  Pallas kernels: 75.1 us -> 83.8 us
  starting transfers between devices: 63.5 us -> 69.4 us
    ppermute x41, waiting for transfers between devices: 98 us -> 88.7 us  [exchange(): return lax.ppermute(value, BOTH, [(i, i ^ mask) for i in range(count)])]
    convert_element_type x4 -> x0, other arithmetic: 6.92 us -> none  [the longest x2 3.47 us: along_z(): add_up([t[m] for t in terms[n]]).astype(BF16)]
    ppermute x41, starting transfers between devices: 40.4 us -> 46.6 us  [exchange(): return lax.ppermute(value, BOTH, [(i, i ^ mask) for i in range(count)])]
    pallas_call x1 -> x3, Pallas kernels: 3.75 us -> 9.84 us  [combine(): pl.pallas_call(functools.partial(combine_kernel, jobs, tails), out_shape=...]
    another operation x11 -> x3, other arithmetic: 6.12 us -> 1.01 us  [in_order(): return jnp.stack([low, high], axis=axis)]
    another operation x7 -> x8, other arithmetic: 2.66 us -> 7.09 us  [the longest x4 3.85 us: second_side(): self.b = jnp.stack([self.b, self.got[1]])]
    pallas_call x0 -> x2, Pallas kernels: none -> 2.99 us  [the longest x1 2.26 us: along_z(): pl.pallas_call(turn_kernel, out_shape=(*(tall,) * 3, jax.ShapeDtypeStruct...]
  transfers between devices with their start and end apart: 45 -> 45, of which waited for: 22 -> 21; matrix products, arithmetic and copies ran while one was open for 11% -> 8% of each run, Pallas kernels for 19% -> 22%
where the time goes in v1:
time: 270 us; the launch traced here: 269 us
  waiting for transfers between devices  89.8 us (33%)
  Pallas kernels  83.8 us (31%)
  starting transfers between devices  69.4 us (26%)
  other arithmetic  14.5 us (5%)
  local copies, waits for them, and re-layouts  9.59 us (4%)
    ppermute x41, waiting for transfers between devices, exchange(): return lax.ppermute(value, BOTH, [(i, i ^ mask) for i in range(count)])  88.7 us
    pallas_call x4, Pallas kernels, run(): pl.pallas_call(body, out_shape=(*(pltpu.HBM(o.shape, o.dtype) for o in ou...  67.7 us
    ppermute x41, starting transfers between devices, exchange(): return lax.ppermute(value, BOTH, [(i, i ^ mask) for i in range(count)])  46.6 us
    pallas_call x3, Pallas kernels, combine(): pl.pallas_call(functools.partial(combine_kernel, jobs, tails), out_shape=...  9.84 us
    all_to_all x1, starting transfers between devices, collect_start(): return lax.all_to_all(pieces, BOTH, split_axis=0, concat_axis=0, tiled=True)  6 us
    all_to_all x1, starting transfers between devices, collect_start_back(): return lax.all_to_all(chosen, 'dp', split_axis=0, concat_axis=0, tiled=True)  5.96 us
    all_to_all x1, starting transfers between devices, deal_finish(): got = lax.all_to_all(chosen, BOTH, split_axis=0, concat_axis=0, tiled=True)  5.76 us
  transfers between devices with their start and end apart: 45, of which 21 were waited for; matrix products, arithmetic and copies ran while one was open for 8% of the time, Pallas kernels for 22%

profile of v1, /device:TPU:0, one launch (start us, length us, event | category | flops | bytes accessed | tf_op | source)
XLA Modules:
  0.0 268.5 jit_solution(813716201140823654)
XLA Ops:
  10.6 3.6 %collective-permute-done.4 = f32[6,384]{1,0:T(8,128)S(1)} collective-permute-done((f32[6,384]{1,0:T(8,128)S(1)}, f32[6,384]{1,0:T(8,128)S(1)}, u32[]{:S(2)}, u32[]{:S(2)}) %collective-permute-start.4) | collective-permute-done | bytes 9248 | tf_op jit(solution)/shard_map/ppermute | solution.py:53
  24.3 4.7 %collective-permute-done.7 = bf16[2,48,1536]{2,1,0:T(8,128)(2,1)S(1)} collective-permute-done((bf16[2,48,1536]{2,1,0:T(8,128)(2,1)S(1)}, bf16[2,48,1536]{2,1,0:T(8,128)(2,1)S(1)}, u32[]{:S(2)}, u32[]{:S(2)}) %collective-permute-start.7) | collective-permute-done | bytes 294944 | tf_op jit(solution)/shard_map/ppermute | solution.py:53
  28.9 6.5 %collective-permute-done.8 = bf16[2,48,1536]{2,1,0:T(8,128)(2,1)S(1)} collective-permute-done((bf16[2,48,1536]{2,1,0:T(8,128)(2,1)S(1)}, bf16[2,48,1536]{2,1,0:T(8,128)(2,1)S(1)}, u32[]{:S(2)}, u32[]{:S(2)}) %collective-permute-start.8) | collective-permute-done | bytes 294944 | tf_op jit(solution)/shard_map/ppermute | solution.py:53
  41.5 5.8 %collective-permute-done.12 = bf16[2,48,1536]{2,1,0:T(8,128)(2,1)S(1)} collective-permute-done((bf16[2,48,1536]{2,1,0:T(8,128)(2,1)S(1)}, bf16[2,48,1536]{2,1,0:T(8,128)(2,1)S(1)}, u32[]{:S(2)}, u32[]{:S(2)}) %collective-permute-start.12) | collective-permute-done | bytes 294944 | tf_op jit(solution)/shard_map/ppermute | solution.py:53
  56.7 5.0 %all-to-all-start = ((bf16[16,32,768]{2,1,0:T(8,128)(2,1)}), bf16[16,32,768]{2,1,0:T(8,128)(2,1)S(1)}, u32[]{:S(2)}, u32[]{:S(2)}) async-start(bf16[16,32,768]{2,1,0:T(8,128)(2,1)} %bitcast.82), calls=%async_computation | async-start | bytes 1572864 | tf_op jit(solution)/shard_map/all_to_all | solution.py:782
  61.8 4.1 %collective-permute-done.17 = bf16[4,48,1536]{2,1,0:T(8,128)(2,1)} collective-permute-done((bf16[4,48,1536]{2,1,0:T(8,128)(2,1)}, bf16[4,48,1536]{2,1,0:T(8,128)(2,1)}, u32[]{:S(2)}, u32[]{:S(2)}) %collective-permute-start.17) | collective-permute-done | bytes 589856 | tf_op jit(solution)/shard_map/ppermute | solution.py:53
  65.9 6.5 %collective-permute-done.16 = bf16[4,48,1536]{2,1,0:T(8,128)(2,1)} collective-permute-done((bf16[4,48,1536]{2,1,0:T(8,128)(2,1)}, bf16[4,48,1536]{2,1,0:T(8,128)(2,1)}, u32[]{:S(2)}, u32[]{:S(2)}) %collective-permute-start.16) | collective-permute-done | bytes 589856 | tf_op jit(solution)/shard_map/ppermute | solution.py:53
  82.2 5.8 %all-to-all-start.1 = ((bf16[32,16,768]{2,1,0:T(8,128)(2,1)}), bf16[32,16,768]{2,1,0:T(8,128)(2,1)}, u32[]{:S(2)}, u32[]{:S(2)}) async-start(bf16[32,16,768]{2,1,0:T(8,128)(2,1)} %pick.2), calls=%async_computation.1 | async-start | bytes 1572864 | tf_op jit(solution)/shard_map/all_to_all | solution.py:791
  88.2 15.5 %attend.1 = (bf16[512,768]{1,0:T(8,128)(2,1)}, bf16[512,768]{1,0:T(8,128)(2,1)}, bf16[512,768]{1,0:T(8,128)(2,1)}, bf16[512,768]{1,0:T(8,128)(2,1)}, f32[512,128...) custom-call(s32[5]{0:T(128)S(1)} %stack.129.scalars, ...), custom_call_target="tpu_custom_call" | custom-call | flops 300000000 | bytes 900000 | tf_op jit(solution)/shard_map/attend/pallas_call | solution.py:502
  103.7 4.6 %collective-permute-done.19.refs_11_ = bf16[2,4,48,1536]{3,2,1,0:T(8,128)(2,1)} collective-permute-done((bf16[2,4,48,1536]{3,2,1,0:T(8,128)(2,1)}, bf16[2,4,48,1536]{3,2,1,0:T(8,128)(2,1)}, u32[]{:S(2)}, u32[]{:S(2)}) %collective-permute-start.19) | collective-permute-done | bytes 1179680 | tf_op jit(solution)/shard_map/ppermute | solution.py:53
  108.3 4.2 %collective-permute-done.18.refs_7_ = bf16[2,4,48,1536]{3,2,1,0:T(8,128)(2,1)S(1)} collective-permute-done((bf16[2,4,48,1536]{3,2,1,0:T(8,128)(2,1)S(1)}, bf16[2,4,48,1536]{3,2,1,0:T(8,128)(2,1)S(1)}, u32[]{:S(2)}, u32[]{:S(2)}) %collective-permute-start.18) | collective-permute-done | bytes 1179680 | tf_op jit(solution)/shard_map/ppermute | solution.py:53
  117.4 23.2 %middle.1 = (bf16[16,2,16,768]{3,2,1,0:T(8,128)(2,1)}, bf16[512,3072]{1,0:T(8,128)(2,1)}, bf16[2,2,2,4,48,1536]{5,4,3,2,1,0:T(8,128)(2,1)}, bf16[2,2,2,4,48,1536...) custom-call(s32[5]{0:T(128)S(1)} %stack.129.scalars, ...), custom_call_target="tpu_custom_call" | custom-call | flops 480000000 | bytes 1440000 | tf_op jit(solution)/shard_map/middle/pallas_call | solution.py:502
  140.8 6.0 %all-to-all-start.2 = ((bf16[32,16,768]{2,1,0:T(8,128)(2,1)}), bf16[32,16,768]{2,1,0:T(8,128)(2,1)S(1)}, u32[]{:S(2)}, u32[]{:S(2)}) async-start(bf16[32,16,768]{2,1,0:T(8,128)(2,1)} %bitcast.88), calls=%async_computation.2 | async-start | bytes 1572864 | tf_op jit(solution)/shard_map/all_to_all | solution.py:798
  148.9 3.6 %first_side.1 = (bf16[384,1536]{1,0:T(8,128)(2,1)}, bf16[384,1536]{1,0:T(8,128)(2,1)}) custom-call(bf16[2,2,8,48,1536]{4,3,2,1,0:T(8,128)(2,1)} %bitcast.78, bf16[2,2,8,48,1536]{4,3,2,1,0:T(8,128)(2,1)} %bitcast.25.refs_1_), custom_call_target="tpu_custom_call" | custom-call | flops 60000000 | bytes 180000 | tf_op jit(solution)/shard_map/first_side/pallas_call | solution.py:708
  157.4 10.0 %normed.1 = (f32[512,768]{1,0:T(8,128)S(1)}, bf16[512,768]{1,0:T(8,128)(2,1)S(1)}, bf16[512,768]{1,0:T(8,128)(2,1)S(1)}, f32[3,768]{1,0:T(4,128)S(1)}) custom-call(s32[5]{0:T(128)S(1)} %stack.129.scalars, bf16[512,3072]{1,0:T(8,128)(2,1)} %get-tuple-element.165.refs_0_, f32[512,768]{1,0:T(8,128)S(1)} %get-tuple-element.166.refs_1_, ...), custom_call_target="tpu_custom_call" | custom-call | flops 160000000 | bytes 480000 | tf_op jit(solution)/shard_map/normed/pallas_call | solution.py:502
  167.4 18.9 %last.1 = (bf16[256,768]{1,0:T(8,128)(2,1)}, bf16[256,768]{1,0:T(8,128)(2,1)}, bf16[4,4,48,1536]{3,2,1,0:T(8,128)(2,1)}, bf16[4,4,48,1536]{3,2,1,0:T(8,128)(2,1)}, f32[2,768]{1,0:T(2,128)S(1)}) custom-call(s32[5]{0:T(128)S(1)} %stack.129.scalars, bf16[512,768]{1,0:T(8,128)(2,1)S(1)} %get-tuple-element.168.refs_0_, ...), custom_call_target="tpu_custom_call" | custom-call | flops 400000000 | bytes 1200000 | tf_op jit(solution)/shard_map/last/pallas_call | solution.py:502
  192.4 6.0 %all-to-all-start.3 = ((bf16[16,32,768]{2,1,0:T(8,128)(2,1)}), bf16[16,32,768]{2,1,0:T(8,128)(2,1)}, u32[]{:S(2)}, u32[]{:S(2)}) async-start(bf16[16,32,768]{2,1,0:T(8,128)(2,1)} %bitcast.34), calls=%async_computation.3 | async-start | bytes 1572864 | tf_op jit(solution)/shard_map/all_to_all | solution.py:808
  200.6 5.2 %collective-permute-done.29 = bf16[192,1536]{1,0:T(8,128)(2,1)} collective-permute-done((bf16[192,1536]{1,0:T(8,128)(2,1)}, bf16[192,1536]{1,0:T(8,128)(2,1)}, u32[]{:S(2)}, u32[]{:S(2)}) %collective-permute-start.29) | collective-permute-done | bytes 589856 | tf_op jit(solution)/shard_map/ppermute | solution.py:53
  205.7 5.7 %collective-permute-done.30 = bf16[192,1536]{1,0:T(8,128)(2,1)} collective-permute-done((bf16[192,1536]{1,0:T(8,128)(2,1)}, bf16[192,1536]{1,0:T(8,128)(2,1)}, u32[]{:S(2)}, u32[]{:S(2)}) %collective-permute-start.30) | collective-permute-done | bytes 589856 | tf_op jit(solution)/shard_map/ppermute | solution.py:53
  218.1 4.0 %collective-permute-start.35 = (bf16[96,1536]{1,0:T(8,128)(2,1)}, bf16[96,1536]{1,0:T(8,128)(2,1)S(1)}, u32[]{:S(2)}, u32[]{:S(2)}) collective-permute-start(bf16[96,1536]{1,0:T(8,128)(2,1)} %get-tuple-element.201), channel_id=1, source_target_pairs={{0,16},{1,17},{2,18},{3,19},{4,20},{5,21},{6,22},{7,23},{8,24},{9,... | collective-permute-start | bytes 884744 | tf_op jit(solution)/shard_map/ppermute | solution.py:53
  222.2 6.0 %collective-permute-done.34 = bf16[96,1536]{1,0:T(8,128)(2,1)S(1)} collective-permute-done((bf16[96,1536]{1,0:T(8,128)(2,1)}, bf16[96,1536]{1,0:T(8,128)(2,1)S(1)}, u32[]{:S(2)}, u32[]{:S(2)}) %collective-permute-start.34) | collective-permute-done | bytes 294944 | tf_op jit(solution)/shard_map/ppermute | solution.py:53
  231.3 9.2 %collective-permute-done.35 = bf16[96,1536]{1,0:T(8,128)(2,1)S(1)} collective-permute-done((bf16[96,1536]{1,0:T(8,128)(2,1)}, bf16[96,1536]{1,0:T(8,128)(2,1)S(1)}, u32[]{:S(2)}, u32[]{:S(2)}) %collective-permute-start.35) | collective-permute-done | bytes 294944 | tf_op jit(solution)/shard_map/ppermute | solution.py:53
  245.0 3.4 %collective-permute-start.38 = (bf16[64,1536]{1,0:T(8,128)(2,1)S(1)}, bf16[64,1536]{1,0:T(8,128)(2,1)S(1)}, u32[]{:S(2)}, u32[]{:S(2)}) collective-permute-start(bf16[64,1536]{1,0:T(8,128)(2,1)S(1)} %get-tuple-element.214), channel_id=1, source_target_pairs={{0,8},{1,9},{2,10},{3,11},{4,12},{5,13},{6,14},{7,15},{8,0},{9,1},... | collective-permute-start | bytes 589832 | tf_op jit(solution)/shard_map/ppermute | solution.py:53
  257.0 7.1 %collective-permute-done.39.second = bf16[64,1536]{1,0:T(8,128)(2,1)S(1)} collective-permute-done((bf16[64,1536]{1,0:T(8,128)(2,1)S(1)}, bf16[64,1536]{1,0:T(8,128)(2,1)S(1)}, u32[]{:S(2)}, u32[]{:S(2)}) %collective-permute-start.39) | collective-permute-done | bytes 196640 | tf_op jit(solution)/shard_map/ppermute | solution.py:53
  (197 shorter events, 92.6 us)
Async XLA Ops:
  1.8 19.5 %collective-permute-start.3 = (bf16[256,768]{1,0:T(8,128)(2,1)S(1)}, bf16[256,768]{1,0:T(8,128)(2,1)S(1)}, u32[]{:S(2)}, u32[]{:S(2)}) collective-permute-start(bf16[256,768]{1,0:T(8,128)(2,1)S(1)} %dynamic-slice_bitcast_fusion), channel_id=1, source_target_pairs={{0,1},{1,0},{2,3},{3,2},{4,5},{5,4},{6,7},{7,6},{8,9},{9,8},{10,11... | collective-permute-start | bytes 1179656 | tf_op jit(solution)/shard_map/ppermute | solution.py:53
  16.0 19.4 %collective-permute-start.8 = (bf16[2,48,1536]{2,1,0:T(8,128)(2,1)S(1)}, bf16[2,48,1536]{2,1,0:T(8,128)(2,1)S(1)}, u32[]{:S(2)}, u32[]{:S(2)}) collective-permute-start(bf16[2,48,1536]{2,1,0:T(8,128)(2,1)S(1)} %pad_maximum_fusion.12), channel_id=1, source_target_pairs={{0,16},{1,17},{2,18},{3,19},{4,20},{5,21},{6,22},{7,23},{8,24},{9,... | collective-permute-start | bytes 884744 | tf_op jit(solution)/shard_map/ppermute | solution.py:53
  40.9 20.8 %collective-permute-start.9 = (bf16[2,4,48,768]{3,2,1,0:T(8,128)(2,1)}, bf16[2,4,48,768]{3,2,1,0:T(8,128)(2,1)}, u32[]{:S(2)}, u32[]{:S(2)}) collective-permute-start(bf16[2,4,48,768]{3,2,1,0:T(8,128)(2,1)} %pad_maximum_fusion.6.refs_3_.refs_10_), channel_id=1, source_target_pairs={{0,2},{1,3},{2,0},{3,1},{4,6},{5,7},{6,4},{7,5},{8,10},{9,11},{10,... | collective-permute-start | bytes 1769480 | tf_op jit(solution)/shard_map/ppermute | solution.py:53
  54.6 17.7 %collective-permute-start.16 = (bf16[4,48,1536]{2,1,0:T(8,128)(2,1)}, bf16[4,48,1536]{2,1,0:T(8,128)(2,1)}, u32[]{:S(2)}, u32[]{:S(2)}) collective-permute-start(bf16[4,48,1536]{2,1,0:T(8,128)(2,1)} %get-tuple-element.245), channel_id=1, source_target_pairs={{0,4},{1,5},{2,6},{3,7},{4,0},{5,1},{6,2},{7,3},{8,12},{9,13},{10,... | collective-permute-start | bytes 1769480 | tf_op jit(solution)/shard_map/ppermute | solution.py:53
  55.2 17.2 %collective-permute-start.13 = (bf16[2,4,48,768]{3,2,1,0:T(8,128)(2,1)S(1)}, bf16[2,4,48,768]{3,2,1,0:T(8,128)(2,1)}, u32[]{:S(2)}, u32[]{:S(2)}) collective-permute-start(bf16[2,4,48,768]{3,2,1,0:T(8,128)(2,1)S(1)} %collective-permute-done.10.refs_5_.refs_12_), channel_id=1, source_target_pairs={{0,2},{1,3},{2,0},{3,1},{4,6},{5,7},{6,4},{7,5},{8,10},{9,11},{10,... | collective-permute-start | bytes 1769480 | tf_op jit(solution)/shard_map/ppermute | solution.py:53
  55.2 17.2 %collective-permute-start.15 = (bf16[2,4,48,768]{3,2,1,0:T(8,128)(2,1)S(1)}, bf16[2,4,48,768]{3,2,1,0:T(8,128)(2,1)S(1)}, u32[]{:S(2)}, u32[]{:S(2)}) collective-permute-start(bf16[2,4,48,768]{3,2,1,0:T(8,128)(2,1)S(1)} %collective-permute-done.11.refs_9_.refs_11_.refs_16_), channel_id=1, source_target_pairs={{0,2},{1,3},{2,0},{3,1},{4,6},{5,7},{6,4},{7,5},{8,10},{9,11},{10,... | collective-permute-start | bytes 1769480 | tf_op jit(solution)/shard_map/ppermute | solution.py:53
  56.7 23.8 %all-to-all-start = ((bf16[16,32,768]{2,1,0:T(8,128)(2,1)}), bf16[16,32,768]{2,1,0:T(8,128)(2,1)S(1)}, u32[]{:S(2)}, u32[]{:S(2)}) async-start(bf16[16,32,768]{2,1,0:T(8,128)(2,1)} %bitcast.82), calls=%async_computation | async-start | bytes 1572864 | tf_op jit(solution)/shard_map/all_to_all | solution.py:782
  75.0 33.3 %collective-permute-start.19 = (bf16[2,4,48,1536]{3,2,1,0:T(8,128)(2,1)}, bf16[2,4,48,1536]{3,2,1,0:T(8,128)(2,1)}, u32[]{:S(2)}, u32[]{:S(2)}) collective-permute-start(bf16[2,4,48,1536]{3,2,1,0:T(8,128)(2,1)} %pad_maximum_fusion.1.refs_9_), channel_id=1, source_target_pairs={{0,4},{1,5},{2,6},{3,7},{4,0},{5,1},{6,2},{7,3},{8,12},{9,13},{10,... | collective-permute-start | bytes 3538952 | tf_op jit(solution)/shard_map/ppermute | solution.py:53
  75.0 33.3 %collective-permute-start.21 = (bf16[2,4,48,1536]{3,2,1,0:T(8,128)(2,1)}, bf16[2,4,48,1536]{3,2,1,0:T(8,128)(2,1)}, u32[]{:S(2)}, u32[]{:S(2)}) collective-permute-start(bf16[2,4,48,1536]{3,2,1,0:T(8,128)(2,1)} %pad_maximum_fusion.1.refs_9_), channel_id=1, source_target_pairs={{0,2},{1,3},{2,0},{3,1},{4,6},{5,7},{6,4},{7,5},{8,10},{9,11},{10,... | collective-permute-start | bytes 3538952 | tf_op jit(solution)/shard_map/ppermute | solution.py:53
  76.3 36.2 %collective-permute-start.18 = (bf16[2,4,48,1536]{3,2,1,0:T(8,128)(2,1)S(1)}, bf16[2,4,48,1536]{3,2,1,0:T(8,128)(2,1)S(1)}, u32[]{:S(2)}, u32[]{:S(2)}) collective-permute-start(bf16[2,4,48,1536]{3,2,1,0:T(8,128)(2,1)S(1)} %pad_maximum_fusion.refs_5_), channel_id=1, source_target_pairs={{0,1},{1,0},{2,3},{3,2},{4,5},{5,4},{6,7},{7,6},{8,9},{9,8},{10,11... | collective-permute-start | bytes 3538952 | tf_op jit(solution)/shard_map/ppermute | solution.py:53
  77.9 34.6 %collective-permute-start.20 = (bf16[2,4,48,1536]{3,2,1,0:T(8,128)(2,1)S(1)}, bf16[2,4,48,1536]{3,2,1,0:T(8,128)(2,1)}, u32[]{:S(2)}, u32[]{:S(2)}) collective-permute-start(bf16[2,4,48,1536]{3,2,1,0:T(8,128)(2,1)S(1)} %pad_maximum_fusion.refs_5_), channel_id=1, source_target_pairs={{0,2},{1,3},{2,0},{3,1},{4,6},{5,7},{6,4},{7,5},{8,10},{9,11},{10,... | collective-permute-start | bytes 3538952 | tf_op jit(solution)/shard_map/ppermute | solution.py:53
  82.2 35.1 %all-to-all-start.1 = ((bf16[32,16,768]{2,1,0:T(8,128)(2,1)}), bf16[32,16,768]{2,1,0:T(8,128)(2,1)}, u32[]{:S(2)}, u32[]{:S(2)}) async-start(bf16[32,16,768]{2,1,0:T(8,128)(2,1)} %pick.2), calls=%async_computation.1 | async-start | bytes 1572864 | tf_op jit(solution)/shard_map/all_to_all | solution.py:791
  140.8 45.5 %all-to-all-start.2 = ((bf16[32,16,768]{2,1,0:T(8,128)(2,1)}), bf16[32,16,768]{2,1,0:T(8,128)(2,1)S(1)}, u32[]{:S(2)}, u32[]{:S(2)}) async-start(bf16[32,16,768]{2,1,0:T(8,128)(2,1)} %bitcast.88), calls=%async_computation.2 | async-start | bytes 1572864 | tf_op jit(solution)/shard_map/all_to_all | solution.py:798
  152.6 33.8 %collective-permute-start.25 = (bf16[384,1536]{1,0:T(8,128)(2,1)}, bf16[384,1536]{1,0:T(8,128)(2,1)}, u32[]{:S(2)}, u32[]{:S(2)}) collective-permute-start(bf16[384,1536]{1,0:T(8,128)(2,1)} %get-tuple-element.185), channel_id=1, source_target_pairs={{0,4},{1,5},{2,6},{3,7},{4,0},{5,1},{6,2},{7,3},{8,12},{9,13},{10,... | collective-permute-start | bytes 3538952 | tf_op jit(solution)/shard_map/ppermute | solution.py:53
  154.7 31.7 %collective-permute-start.26 = (bf16[384,1536]{1,0:T(8,128)(2,1)}, bf16[384,1536]{1,0:T(8,128)(2,1)}, u32[]{:S(2)}, u32[]{:S(2)}) collective-permute-start(bf16[384,1536]{1,0:T(8,128)(2,1)} %get-tuple-element.186), channel_id=1, source_target_pairs={{0,1},{1,0},{2,3},{3,2},{4,5},{5,4},{6,7},{7,6},{8,9},{9,8},{10,11... | collective-permute-start | bytes 3538952 | tf_op jit(solution)/shard_map/ppermute | solution.py:53
  190.1 15.6 %collective-permute-start.29 = (bf16[192,1536]{1,0:T(8,128)(2,1)}, bf16[192,1536]{1,0:T(8,128)(2,1)}, u32[]{:S(2)}, u32[]{:S(2)}) collective-permute-start(bf16[192,1536]{1,0:T(8,128)(2,1)} %get-tuple-element.193), channel_id=1, source_target_pairs={{0,1},{1,0},{2,3},{3,2},{4,5},{5,4},{6,7},{7,6},{8,9},{9,8},{10,11... | collective-permute-start | bytes 1769480 | tf_op jit(solution)/shard_map/ppermute | solution.py:53
  190.8 20.6 %collective-permute-start.30 = (bf16[192,1536]{1,0:T(8,128)(2,1)}, bf16[192,1536]{1,0:T(8,128)(2,1)}, u32[]{:S(2)}, u32[]{:S(2)}) collective-permute-start(bf16[192,1536]{1,0:T(8,128)(2,1)} %get-tuple-element.194), channel_id=1, source_target_pairs={{0,4},{1,5},{2,6},{3,7},{4,0},{5,1},{6,2},{7,3},{8,12},{9,13},{10,... | collective-permute-start | bytes 1769480 | tf_op jit(solution)/shard_map/ppermute | solution.py:53
  192.4 38.9 %all-to-all-start.3 = ((bf16[16,32,768]{2,1,0:T(8,128)(2,1)}), bf16[16,32,768]{2,1,0:T(8,128)(2,1)}, u32[]{:S(2)}, u32[]{:S(2)}) async-start(bf16[16,32,768]{2,1,0:T(8,128)(2,1)} %bitcast.34), calls=%async_computation.3 | async-start | bytes 1572864 | tf_op jit(solution)/shard_map/all_to_all | solution.py:808
  211.4 29.1 %collective-permute-start.31 = (bf16[208,1536]{1,0:T(8,128)(2,1)S(1)}, bf16[208,1536]{1,0:T(8,128)(2,1)S(1)}, u32[]{:S(2)}, u32[]{:S(2)}) collective-permute-start(bf16[208,1536]{1,0:T(8,128)(2,1)S(1)} %get-tuple-element.195), channel_id=1, source_target_pairs={{0,1},{1,0},{2,3},{3,2},{4,5},{5,4},{6,7},{7,6},{8,9},{9,8},{10,11... | collective-permute-start | bytes 1916936 | tf_op jit(solution)/shard_map/ppermute | solution.py:53
  213.0 27.5 %collective-permute-start.32 = (bf16[208,1536]{1,0:T(8,128)(2,1)S(1)}, bf16[208,1536]{1,0:T(8,128)(2,1)}, u32[]{:S(2)}, u32[]{:S(2)}) collective-permute-start(bf16[208,1536]{1,0:T(8,128)(2,1)S(1)} %get-tuple-element.196), channel_id=1, source_target_pairs={{0,4},{1,5},{2,6},{3,7},{4,0},{5,1},{6,2},{7,3},{8,12},{9,13},{10,... | collective-permute-start | bytes 1916936 | tf_op jit(solution)/shard_map/ppermute | solution.py:53
  213.0 29.8 %collective-permute-start.33 = (bf16[208,1536]{1,0:T(8,128)(2,1)S(1)}, bf16[208,1536]{1,0:T(8,128)(2,1)}, u32[]{:S(2)}, u32[]{:S(2)}) collective-permute-start(bf16[208,1536]{1,0:T(8,128)(2,1)S(1)} %get-tuple-element.197), channel_id=1, source_target_pairs={{0,5},{1,4},{2,7},{3,6},{4,1},{5,0},{6,3},{7,2},{8,13},{9,12},{10,... | collective-permute-start | bytes 1916936 | tf_op jit(solution)/shard_map/ppermute | solution.py:53
  218.1 22.4 %collective-permute-start.35 = (bf16[96,1536]{1,0:T(8,128)(2,1)}, bf16[96,1536]{1,0:T(8,128)(2,1)S(1)}, u32[]{:S(2)}, u32[]{:S(2)}) collective-permute-start(bf16[96,1536]{1,0:T(8,128)(2,1)} %get-tuple-element.201), channel_id=1, source_target_pairs={{0,16},{1,17},{2,18},{3,19},{4,20},{5,21},{6,22},{7,23},{8,24},{9,... | collective-permute-start | bytes 884744 | tf_op jit(solution)/shard_map/ppermute | solution.py:53
  248.4 15.7 %collective-permute-start.39 = (bf16[64,1536]{1,0:T(8,128)(2,1)S(1)}, bf16[64,1536]{1,0:T(8,128)(2,1)S(1)}, u32[]{:S(2)}, u32[]{:S(2)}) collective-permute-start(bf16[64,1536]{1,0:T(8,128)(2,1)S(1)} %get-tuple-element.215), channel_id=1, source_target_pairs={{0,16},{1,17},{2,18},{3,19},{4,20},{5,21},{6,22},{7,23},{8,24},{9,... | collective-permute-start | bytes 589832 | tf_op jit(solution)/shard_map/ppermute | solution.py:53
  250.9 16.6 %collective-permute-start.37 = (bf16[256,768]{1,0:T(8,128)(2,1)}, bf16[256,768]{1,0:T(8,128)(2,1)S(1)}, u32[]{:S(2)}, u32[]{:S(2)}) collective-permute-start(bf16[256,768]{1,0:T(8,128)(2,1)} %get-tuple-element.207), channel_id=1, source_target_pairs={{0,1},{1,0},{2,3},{3,2},{4,5},{5,4},{6,7},{7,6},{8,9},{9,8},{10,11... | collective-permute-start | bytes 1179656 | tf_op jit(solution)/shard_map/ppermute | solution.py:53
  (49 other events, 453.8 us)

commit v2 on v1

--- a/solution.py
+++ b/solution.py
@@ -548,16 +548,27 @@
     return rows[:count].astype(F32) + rows[count : 2 * count].astype(F32)
 
 
-def finish_kernel(partial, own, first, second, third, *refs):
-    outs, extra = refs[:-1], refs[-1]
+def finish_kernel(scalars, partial, own, first, second, third, *refs):
+    grads, vectors, extra = refs[:4], refs[4:13], refs[13]
     rows = partial.shape[0]
     last = [r[...].astype(F32) for r in (first, second, third)]
     total = partial[...] + last[0][:rows] + last[1][:rows] + last[2][:rows]
-    cols = outs[0].shape[1]
-    for n, out in enumerate(outs):
+    cols = grads[0].shape[1]
+    for n, out in enumerate(grads):
         out[...] = total[:, n * cols : (n + 1) * cols]
     low = own[...].astype(F32)
     extra[...] = pairs([r[:8] + r[8:] for r in (low, *(v[rows:] for v in last))])
+    features = extra.shape[1] // 2
+    at_y = scalars[AT_Y]
+
+    def put(out, row, start):
+        out[...] = extra[pl.ds(row, 1), pl.ds(pl.multiple_of(start, 128), out.shape[-1])].reshape(out.shape)
+
+    put(vectors[0], 3, at_y * cols)
+    put(vectors[1], 3, features + at_y * cols)
+    put(vectors[3], 4 + at_y, 0)
+    for out, n in zip((vectors[2], *vectors[4:]), (3, 0, 4, 5, 1, 2)):
+        put(out, n // 2, n % 2 * features)
 
 
 def turn_kernel(keep, near, *refs):
@@ -642,80 +653,90 @@
         )(*map(in_hbm, (self.keep, self.near, *self.got)), self.low)
         self.got = [exchange(s, m * Z_BIT) for s, m in zip(sent, (1, 2, 3))]
 
-    def finish(self, count):
+    def finish(self, scalars, unit_cols, features):
         rows, width = self.shape[-2:]
-        shapes = [jax.ShapeDtypeStruct((rows, width // count), F32)] * count
-        *grads, extra = pl.pallas_call(
+        cols = width // 4
+
+        def out(*shape):
+            return jax.ShapeDtypeStruct(shape, F32)
+
+        vectors = [out(n) for n in (cols, cols, features, unit_cols, *(features,) * 5)]
+        return pl.pallas_call(
             finish_kernel,
-            out_shape=(*shapes, jax.ShapeDtypeStruct((8, width), F32)),
-            in_specs=[VMEM] * 5,
-            out_specs=(VMEM,) * (count + 1),
+            out_shape=(*[out(rows, cols)] * 4, *vectors),
+            in_specs=[SMEM] + [VMEM] * 5,
+            out_specs=(VMEM,) * 13,
+            scratch_shapes=[pltpu.VMEM((8, width), F32)],
             compiler_params=params(6),
             cost_estimate=cost(2),
             name="finish",
-        )(self.partial, self.low, *self.got)
-        return grads, extra[: self.extra.shape[0]]
-
-
-def combine_kernel(jobs, tails, *refs):
+        )(scalars, self.partial, self.low, *self.got)
+
+
+def combine_kernel(jobs, *refs):
     refs = list(refs)
 
     def take(n):
         got, refs[:] = refs[:n], refs[n:]
         return got
 
-    arrays = take(1 + max(n for job in jobs for part in job for n, _ in part))
-    rows_in = take(2 if tails else 0)
+    arrays = take(1 + max(n for job in jobs for n, _ in job))
     outs = take(len(jobs))
-    rows_out = take(1 if tails else 0)
     move = Mover(refs.pop())
-    into = [take(len(job)) for job in jobs]
+    into = take(len(jobs))
     copies = [
-        [move(arrays[n].at[at], ref.at[k]) for part, ref in zip(job, some) for k, (n, at) in enumerate(part)]
-        for job, some in zip(jobs, into)
+        [[move(arrays[n].at[(*at, b)], ref.at[k, b]) for k, (n, at) in enumerate(job)] for b in range(ref.shape[1])]
+        for job, ref in zip(jobs, into)
     ]
-    if tails:
-        total = rows_in[0][...] + rows_in[1][...]
-        rows_out[0][...] = total
-        below = split_wide(total)
     sent = []
-    for number, (job, some, made) in enumerate(zip(jobs, into, refs)):
-        wait(copies[number])
-        at = 0
-        for ref in some:
-            terms, blocks, high, _ = ref.shape
-            for b in range(blocks):
-                total = ref[0, b].astype(F32)
-                for k in range(1, terms):
-                    total = total + ref[k, b].astype(F32)
-                made[at : at + high] = total.astype(BF16)
-                at += high
-        if number in tails:
-            made[at:] = below
-        sent.append(move(made, outs[number]))
+    for number, (job, ref, made) in enumerate(zip(jobs, into, refs)):
+        for b, some in enumerate(copies[number]):
+            wait(some)
+            for c in range(ref.shape[2]):
+                total = ref[0, b, c].astype(F32)
+                for k in range(1, len(job)):
+                    total = total + ref[k, b, c].astype(F32)
+                made[b, c] = total.astype(BF16)
+            sent.append(move(made.at[b], outs[number].at[b]))
     wait(sent)
 
 
-def combine(name, us, arrays, jobs, shape, tails=(), rows=()):
-    blocks, high, width = shape
-    outs = [
-        jax.ShapeDtypeStruct((len(job) * blocks * high + (16 if n in tails else 0), width), BF16)
-        for n, job in enumerate(jobs)
-    ]
-    scratch = [pltpu.VMEM((len(part), *shape), BF16) for job in jobs for part in job]
-    scratch += [pltpu.VMEM(out.shape, BF16) for out in outs]
-    copies = sum(len(part) for job in jobs for part in job) + len(jobs)
+def combine(name, us, arrays, jobs, shape):
+    outs = [jax.ShapeDtypeStruct(shape, BF16)] * len(jobs)
+    scratch = [pltpu.VMEM((len(job), *shape), BF16) for job in jobs] + [pltpu.VMEM(shape, BF16)] * len(jobs)
+    copies = shape[0] * (sum(map(len, jobs)) + len(jobs))
     return pl.pallas_call(
-        functools.partial(combine_kernel, jobs, tails),
-        out_shape=[pltpu.HBM(o.shape, o.dtype) for o in outs]
-        + [jax.ShapeDtypeStruct(r.shape, r.dtype) for r in rows[:1]],
-        in_specs=[HBM] * len(arrays) + [VMEM] * len(rows),
-        out_specs=[HBM] * len(outs) + [VMEM] * len(rows[:1]),
+        functools.partial(combine_kernel, jobs),
+        out_shape=[pltpu.HBM(o.shape, o.dtype) for o in outs],
+        in_specs=[HBM] * len(arrays),
+        out_specs=[HBM] * len(outs),
         scratch_shapes=[*scratch, pltpu.SemaphoreType.DMA((copies,))],
         compiler_params=params(12),
         cost_estimate=cost(us),
         name=name,
-    )(*map(in_hbm, arrays), *rows)
+    )(*map(in_hbm, arrays))
+
+
+def along_z_kernel(keep, near, *refs):
+    got, sent = refs[:4], refs[4:7]
+    parts, made = refs[7], refs[8]
+    move = Mover(refs[9])
+    copies = []
+    far = pl.ds(1, 3)
+    for h in range(2):
+        terms = (keep.at[h, 0, 0], near.at[h, 0, 0], got[h].at[0], got[2 + h])
+        copies.append([move(t.at[far], parts.at[h, k]) for k, t in enumerate(terms)])
+    moved = []
+    for h in range(2):
+        wait(copies[h])
+        for m in range(3):
+            total = parts[h, 0, m].astype(F32)
+            for k in range(1, 4):
+                total = total + parts[h, k, m].astype(F32)
+            made[m, h] = total.astype(BF16)
+            if h:
+                moved.append(move(made.at[m], sent[m]))
+    wait(moved)
 
 
 class ScatterTwo:
@@ -726,37 +747,43 @@
         self.got = exchange(self.send, C_BIT)
 
     def first_side(self):
-        self.rows, self.width = self.send.shape[-2:]
-        self.arrays = [a.reshape(2, 2, 8, self.rows, self.width) for a in (self.keep, self.got)]
-        sent = combine(
-            "first_side", 3, self.arrays, [[[(n, (h, 1)) for n in range(2)]] for h in range(2)], (8, self.rows, self.width)
-        )
-        self.got = [exchange(s, m).reshape(8, self.rows, self.width) for s, m in zip(sent, (X_BIT, Y_BIT))]
+        self.arrays = [self.keep, self.got]
+        jobs = [[(n, (h, 1)) for n in range(2)] for h in range(2)]
+        sent = combine("first_side", 3, self.arrays, jobs, self.keep.shape[2:])
+        self.got = [exchange(s, m) for s, m in zip(sent, (X_BIT, Y_BIT))]
 
     def second_side(self):
         self.arrays += self.got
-        far = pl.ds(4, 4)
-        sent = combine(
-            "second_side", 3, self.arrays,
-            [[[(0, (h, 0, far)), (1, (h, 0, far)), (2 + h, (far,))]] for h in range(2)],
-            (4, self.rows, self.width),
-        )
-        self.got = [exchange(s, m).reshape(4, self.rows, self.width) for s, m in zip(sent, (Y_BIT, X_BIT))]
+        blocks = self.keep.shape[3:]
+        jobs = [[(0, (h, 0, 1)), (1, (h, 0, 1)), (2 + h, (1,))] for h in range(2)]
+        arrays = [a.reshape(*a.shape[:-3], 2, 2, *a.shape[-2:]) for a in self.arrays]
+        sent = combine("second_side", 3, arrays, jobs, (2, 2, *blocks[1:]))
+        self.got = [exchange(s, m).reshape(blocks) for s, m in zip(sent, (Y_BIT, X_BIT))]
 
     def along_z(self):
         self.arrays += self.got
-        jobs = [
-            [[(0, (h, 0, at)), (1, (h, 0, at)), (2 + h, (at,)), (4 + h, (at,))] for h in range(2)]
-            for at in (pl.ds(m, 1) for m in (1, 2, 3))
-        ]
-        sent = combine("along_z", 3, self.arrays, jobs, (1, self.rows, self.width))
+        rows, width = self.keep.shape[-2:]
+        out = pltpu.HBM((2, rows, width), BF16)
+        sent = pl.pallas_call(
+            along_z_kernel,
+            out_shape=[out] * 3,
+            in_specs=[HBM] * 6,
+            out_specs=[HBM] * 3,
+            scratch_shapes=[
+                pltpu.VMEM((2, 4, 3, rows, width), BF16), pltpu.VMEM((3, 2, rows, width), BF16),
+                pltpu.SemaphoreType.DMA((11,)),
+            ],
+            compiler_params=params(8),
+            cost_estimate=cost(3),
+            name="along_z",
+        )(*map(in_hbm, self.arrays))
         self.got = [exchange(s, m * Z_BIT) for s, m in zip(sent, (1, 2, 3))]
 
     def total(self):
         sums = []
         for h in range(2):
-            terms = [self.arrays[n][h, 0, 0] for n in range(2)] + [self.arrays[n + h][0] for n in (2, 4)]
-            sums.append(add_up(terms + [g[h * self.rows : (h + 1) * self.rows] for g in self.got]))
+            terms = [self.arrays[n][h, 0, 0, 0] for n in range(2)] + [self.arrays[2 + h][0, 0], self.arrays[4 + h][0]]
+            sums.append(add_up(terms + [g[h] for g in self.got]))
         return sums
 
 
@@ -967,9 +994,10 @@
         input_grad = in_order(at_y, own_grad, exchange(other_grad, Y_BIT))
         head_sum.along_z()
         layer_out = collect_end(layer_out, micro)
-        grads, sums = head_sum.finish(4)
-        grads += wide_sum.total()
-        sums = sums.reshape(-1, features)
+        head_sum.got[0], input_grad = tie(head_sum.got[0], input_grad)
+        results = head_sum.finish(scalars, unit_cols, features)
+        grads = [*results[:4], *wide_sum.total()]
+        vectors = results[4:]
     else:
         layer_out = collect_end(collect_start_back(collect_pick(out, slot_order), micro), micro)
         input_grad = in_order(at_y, own_grad, exchange(other_grad, Y_BIT))
@@ -978,14 +1006,15 @@
         grads += [scatter_whole(wide_grad[0][n], rows, unit_cols) for n in range(2)]
         sums = lax.psum(sums, BOTH)
 
-    def own(vec, width):
-        return lax.dynamic_slice_in_dim(vec, at_y * width, width)
-
-    return (
-        layer_out, input_grad, *grads,
-        own(sums[6], cols), own(sums[7], cols), sums[3], own(sums[8:].reshape(-1), unit_cols), sums[0],
-        sums[4], sums[5], sums[1], sums[2],
-    )
+        def own(vec, width):
+            return lax.dynamic_slice_in_dim(vec, at_y * width, width)
+
+        vectors = (
+            own(sums[6], cols), own(sums[7], cols), sums[3], own(sums[8:].reshape(-1), unit_cols), sums[0],
+            sums[4], sums[5], sums[1], sums[2],
+        )
+
+    return layer_out, input_grad, *grads, *vectors
 
 
 def solution(mesh):

time: 270 us -> 268 us (level)
  no operation moved by 1% of the time
where the time goes in v2:
time: 268 us; the launch traced here: 266 us
  waiting for transfers between devices  88.7 us (33%)
  Pallas kernels  84.1 us (31%)
  starting transfers between devices  68.4 us (26%)
  other arithmetic  15.6 us (6%)
  local copies, waits for them, and re-layouts  7.26 us (3%)
    ppermute x41, waiting for transfers between devices, exchange(): return lax.ppermute(value, BOTH, [(i, i ^ mask) for i in range(count)])  87.6 us
    pallas_call x4, Pallas kernels, run(): pl.pallas_call(body, out_shape=(*(pltpu.HBM(o.shape, o.dtype) for o in ou...  67.8 us
    ppermute x41, starting transfers between devices, exchange(): return lax.ppermute(value, BOTH, [(i, i ^ mask) for i in range(count)])  45.8 us
    pallas_call x2, Pallas kernels, combine(): pl.pallas_call(functools.partial(combine_kernel, jobs), out_shape=[pltpu....  6.38 us
    all_to_all x1, starting transfers between devices, collect_start(): return lax.all_to_all(pieces, BOTH, split_axis=0, concat_axis=0, tiled=True)  6.01 us
    all_to_all x1, starting transfers between devices, collect_start_back(): return lax.all_to_all(chosen, 'dp', split_axis=0, concat_axis=0, tiled=True)  5.88 us
    all_to_all x1, starting transfers between devices, deal_finish(): got = lax.all_to_all(chosen, BOTH, split_axis=0, concat_axis=0, tiled=True)  5.76 us
  transfers between devices with their start and end apart: 45, of which 21 were waited for; matrix products, arithmetic and copies ran while one was open for 8% of the time, Pallas kernels for 22%

profile of v2, /device:TPU:0, one launch (start us, length us, event | category | flops | bytes accessed | tf_op | source)
XLA Modules:
  0.0 265.7 jit_solution(1201155393193989677)
XLA Ops:
  10.6 3.6 %collective-permute-done.4 = f32[6,384]{1,0:T(8,128)S(1)} collective-permute-done((f32[6,384]{1,0:T(8,128)S(1)}, f32[6,384]{1,0:T(8,128)S(1)}, u32[]{:S(2)}, u32[]{:S(2)}) %collective-permute-start.4) | collective-permute-done | bytes 9248 | tf_op jit(solution)/shard_map/ppermute | solution.py:53
  24.3 4.7 %collective-permute-done.7 = bf16[2,48,1536]{2,1,0:T(8,128)(2,1)S(1)} collective-permute-done((bf16[2,48,1536]{2,1,0:T(8,128)(2,1)S(1)}, bf16[2,48,1536]{2,1,0:T(8,128)(2,1)S(1)}, u32[]{:S(2)}, u32[]{:S(2)}) %collective-permute-start.7) | collective-permute-done | bytes 294944 | tf_op jit(solution)/shard_map/ppermute | solution.py:53
  28.9 6.5 %collective-permute-done.8 = bf16[2,48,1536]{2,1,0:T(8,128)(2,1)S(1)} collective-permute-done((bf16[2,48,1536]{2,1,0:T(8,128)(2,1)S(1)}, bf16[2,48,1536]{2,1,0:T(8,128)(2,1)S(1)}, u32[]{:S(2)}, u32[]{:S(2)}) %collective-permute-start.8) | collective-permute-done | bytes 294944 | tf_op jit(solution)/shard_map/ppermute | solution.py:53
  41.4 5.8 %collective-permute-done.12 = bf16[2,48,1536]{2,1,0:T(8,128)(2,1)S(1)} collective-permute-done((bf16[2,48,1536]{2,1,0:T(8,128)(2,1)S(1)}, bf16[2,48,1536]{2,1,0:T(8,128)(2,1)S(1)}, u32[]{:S(2)}, u32[]{:S(2)}) %collective-permute-start.12) | collective-permute-done | bytes 294944 | tf_op jit(solution)/shard_map/ppermute | solution.py:53
  56.7 5.0 %all-to-all-start = ((bf16[16,32,768]{2,1,0:T(8,128)(2,1)}), bf16[16,32,768]{2,1,0:T(8,128)(2,1)S(1)}, u32[]{:S(2)}, u32[]{:S(2)}) async-start(bf16[16,32,768]{2,1,0:T(8,128)(2,1)} %bitcast.95), calls=%async_computation | async-start | bytes 1572864 | tf_op jit(solution)/shard_map/all_to_all | solution.py:809
  61.7 4.1 %collective-permute-done.17 = bf16[4,48,1536]{2,1,0:T(8,128)(2,1)} collective-permute-done((bf16[4,48,1536]{2,1,0:T(8,128)(2,1)}, bf16[4,48,1536]{2,1,0:T(8,128)(2,1)}, u32[]{:S(2)}, u32[]{:S(2)}) %collective-permute-start.17) | collective-permute-done | bytes 589856 | tf_op jit(solution)/shard_map/ppermute | solution.py:53
  65.8 6.5 %collective-permute-done.16 = bf16[4,48,1536]{2,1,0:T(8,128)(2,1)} collective-permute-done((bf16[4,48,1536]{2,1,0:T(8,128)(2,1)}, bf16[4,48,1536]{2,1,0:T(8,128)(2,1)}, u32[]{:S(2)}, u32[]{:S(2)}) %collective-permute-start.16) | collective-permute-done | bytes 589856 | tf_op jit(solution)/shard_map/ppermute | solution.py:53
  82.1 5.8 %all-to-all-start.1 = ((bf16[32,16,768]{2,1,0:T(8,128)(2,1)}), bf16[32,16,768]{2,1,0:T(8,128)(2,1)}, u32[]{:S(2)}, u32[]{:S(2)}) async-start(bf16[32,16,768]{2,1,0:T(8,128)(2,1)} %pick.2), calls=%async_computation.1 | async-start | bytes 1572864 | tf_op jit(solution)/shard_map/all_to_all | solution.py:818
  88.1 15.6 %attend.1 = (bf16[512,768]{1,0:T(8,128)(2,1)}, bf16[512,768]{1,0:T(8,128)(2,1)}, bf16[512,768]{1,0:T(8,128)(2,1)}, bf16[512,768]{1,0:T(8,128)(2,1)}, f32[512,128...) custom-call(s32[5]{0:T(128)S(1)} %stack.129.scalars, ...), custom_call_target="tpu_custom_call" | custom-call | flops 300000000 | bytes 900000 | tf_op jit(solution)/shard_map/attend/pallas_call | solution.py:502
  103.6 4.6 %collective-permute-done.19.refs_11_ = bf16[2,4,48,1536]{3,2,1,0:T(8,128)(2,1)} collective-permute-done((bf16[2,4,48,1536]{3,2,1,0:T(8,128)(2,1)}, bf16[2,4,48,1536]{3,2,1,0:T(8,128)(2,1)}, u32[]{:S(2)}, u32[]{:S(2)}) %collective-permute-start.19) | collective-permute-done | bytes 1179680 | tf_op jit(solution)/shard_map/ppermute | solution.py:53
  108.2 4.2 %collective-permute-done.18.refs_7_ = bf16[2,4,48,1536]{3,2,1,0:T(8,128)(2,1)S(1)} collective-permute-done((bf16[2,4,48,1536]{3,2,1,0:T(8,128)(2,1)S(1)}, bf16[2,4,48,1536]{3,2,1,0:T(8,128)(2,1)S(1)}, u32[]{:S(2)}, u32[]{:S(2)}) %collective-permute-start.18) | collective-permute-done | bytes 1179680 | tf_op jit(solution)/shard_map/ppermute | solution.py:53
  117.3 23.3 %middle.1 = (bf16[16,2,16,768]{3,2,1,0:T(8,128)(2,1)}, bf16[512,3072]{1,0:T(8,128)(2,1)}, bf16[2,2,2,4,48,1536]{5,4,3,2,1,0:T(8,128)(2,1)}, bf16[2,2,2,4,48,1536...) custom-call(s32[5]{0:T(128)S(1)} %stack.129.scalars, ...), custom_call_target="tpu_custom_call" | custom-call | flops 480000000 | bytes 1440000 | tf_op jit(solution)/shard_map/middle/pallas_call | solution.py:502
  140.8 6.0 %all-to-all-start.2 = ((bf16[32,16,768]{2,1,0:T(8,128)(2,1)}), bf16[32,16,768]{2,1,0:T(8,128)(2,1)S(1)}, u32[]{:S(2)}, u32[]{:S(2)}) async-start(bf16[32,16,768]{2,1,0:T(8,128)(2,1)} %bitcast.100), calls=%async_computation.2 | async-start | bytes 1572864 | tf_op jit(solution)/shard_map/all_to_all | solution.py:825
  148.9 3.5 %first_side.1 = (bf16[2,4,48,1536]{3,2,1,0:T(8,128)(2,1)}, bf16[2,4,48,1536]{3,2,1,0:T(8,128)(2,1)}) custom-call(bf16[2,2,2,4,48,1536]{5,4,3,2,1,0:T(8,128)(2,1)} %get-tuple-element.193.refs_0_.keep, bf16[2,2,2,4,48,1536]{5,4,3,2,1,0:T(8,128)(2,1)} %collective-permute-done.24.refs_1_.near), custom_call_target="tpu_custom_call" | custom-call | flops 60000000 | bytes 180000 | tf_op jit(solution)/shard_map/first_side/pallas_call | solution.py:708
  157.2 10.0 %normed.1 = (f32[512,768]{1,0:T(8,128)S(1)}, bf16[512,768]{1,0:T(8,128)(2,1)S(1)}, bf16[512,768]{1,0:T(8,128)(2,1)S(1)}, f32[3,768]{1,0:T(4,128)S(1)}) custom-call(s32[5]{0:T(128)S(1)} %stack.129.scalars, bf16[512,3072]{1,0:T(8,128)(2,1)} %get-tuple-element.175.refs_0_, f32[512,768]{1,0:T(8,128)S(1)} %get-tuple-element.176.refs_1_, ...), custom_call_target="tpu_custom_call" | custom-call | flops 160000000 | bytes 480000 | tf_op jit(solution)/shard_map/normed/pallas_call | solution.py:502
  167.3 18.9 %last.1 = (bf16[256,768]{1,0:T(8,128)(2,1)}, bf16[256,768]{1,0:T(8,128)(2,1)}, bf16[4,4,48,1536]{3,2,1,0:T(8,128)(2,1)}, bf16[4,4,48,1536]{3,2,1,0:T(8,128)(2,1)}, f32[2,768]{1,0:T(2,128)S(1)}) custom-call(s32[5]{0:T(128)S(1)} %stack.129.scalars, bf16[512,768]{1,0:T(8,128)(2,1)S(1)} %get-tuple-element.178.refs_0_, ...), custom_call_target="tpu_custom_call" | custom-call | flops 400000000 | bytes 1200000 | tf_op jit(solution)/shard_map/last/pallas_call | solution.py:502
  192.3 5.9 %all-to-all-start.3 = ((bf16[16,32,768]{2,1,0:T(8,128)(2,1)}), bf16[16,32,768]{2,1,0:T(8,128)(2,1)}, u32[]{:S(2)}, u32[]{:S(2)}) async-start(bf16[16,32,768]{2,1,0:T(8,128)(2,1)} %bitcast.34), calls=%async_computation.3 | async-start | bytes 1572864 | tf_op jit(solution)/shard_map/all_to_all | solution.py:835
  201.3 4.2 %collective-permute-done.29 = bf16[2,2,48,1536]{3,2,1,0:T(8,128)(2,1)} collective-permute-done((bf16[2,2,48,1536]{3,2,1,0:T(8,128)(2,1)}, bf16[2,2,48,1536]{3,2,1,0:T(8,128)(2,1)}, u32[]{:S(2)}, u32[]{:S(2)}) %collective-permute-start.29) | collective-permute-done | bytes 589856 | tf_op jit(solution)/shard_map/ppermute | solution.py:53
  205.5 5.7 %collective-permute-done.30 = bf16[2,2,48,1536]{3,2,1,0:T(8,128)(2,1)} collective-permute-done((bf16[2,2,48,1536]{3,2,1,0:T(8,128)(2,1)}, bf16[2,2,48,1536]{3,2,1,0:T(8,128)(2,1)}, u32[]{:S(2)}, u32[]{:S(2)}) %collective-permute-start.30) | collective-permute-done | bytes 589856 | tf_op jit(solution)/shard_map/ppermute | solution.py:53
  217.8 4.0 %collective-permute-start.35 = (bf16[2,48,1536]{2,1,0:T(8,128)(2,1)}, bf16[2,48,1536]{2,1,0:T(8,128)(2,1)}, u32[]{:S(2)}, u32[]{:S(2)}) collective-permute-start(bf16[2,48,1536]{2,1,0:T(8,128)(2,1)} %get-tuple-element.211), channel_id=1, source_target_pairs={{0,16},{1,17},{2,18},{3,19},{4,20},{5,21},{6,22},{7,23},{8,24},{9,... | collective-permute-start | bytes 884744 | tf_op jit(solution)/shard_map/ppermute | solution.py:53
  221.8 6.1 %collective-permute-done.34 = bf16[2,48,1536]{2,1,0:T(8,128)(2,1)S(1)} collective-permute-done((bf16[2,48,1536]{2,1,0:T(8,128)(2,1)}, bf16[2,48,1536]{2,1,0:T(8,128)(2,1)S(1)}, u32[]{:S(2)}, u32[]{:S(2)}) %collective-permute-start.34) | collective-permute-done | bytes 294944 | tf_op jit(solution)/shard_map/ppermute | solution.py:53
  231.0 9.3 %collective-permute-done.35 = bf16[2,48,1536]{2,1,0:T(8,128)(2,1)} collective-permute-done((bf16[2,48,1536]{2,1,0:T(8,128)(2,1)}, bf16[2,48,1536]{2,1,0:T(8,128)(2,1)}, u32[]{:S(2)}, u32[]{:S(2)}) %collective-permute-start.35) | collective-permute-done | bytes 294944 | tf_op jit(solution)/shard_map/ppermute | solution.py:53
  245.5 3.6 %collective-permute-start.37 = (bf16[64,1536]{1,0:T(8,128)(2,1)S(1)}, bf16[64,1536]{1,0:T(8,128)(2,1)S(1)}, u32[]{:S(2)}, u32[]{:S(2)}) collective-permute-start(bf16[64,1536]{1,0:T(8,128)(2,1)S(1)} %get-tuple-element.220), channel_id=1, source_target_pairs={{0,8},{1,9},{2,10},{3,11},{4,12},{5,13},{6,14},{7,15},{8,0},{9,1},... | collective-permute-start | bytes 589832 | tf_op jit(solution)/shard_map/ppermute | solution.py:53
  257.3 6.9 %collective-permute-done.39.second = bf16[64,1536]{1,0:T(8,128)(2,1)S(1)} collective-permute-done((bf16[64,1536]{1,0:T(8,128)(2,1)S(1)}, bf16[64,1536]{1,0:T(8,128)(2,1)S(1)}, u32[]{:S(2)}, u32[]{:S(2)}) %collective-permute-start.39) | collective-permute-done | bytes 196640 | tf_op jit(solution)/shard_map/ppermute | solution.py:53
  (192 shorter events, 90.6 us)
Async XLA Ops:
  1.8 19.5 %collective-permute-start.3 = (bf16[256,768]{1,0:T(8,128)(2,1)S(1)}, bf16[256,768]{1,0:T(8,128)(2,1)S(1)}, u32[]{:S(2)}, u32[]{:S(2)}) collective-permute-start(bf16[256,768]{1,0:T(8,128)(2,1)S(1)} %dynamic-slice_bitcast_fusion), channel_id=1, source_target_pairs={{0,1},{1,0},{2,3},{3,2},{4,5},{5,4},{6,7},{7,6},{8,9},{9,8},{10,11... | collective-permute-start | bytes 1179656 | tf_op jit(solution)/shard_map/ppermute | solution.py:53
  16.0 19.4 %collective-permute-start.8 = (bf16[2,48,1536]{2,1,0:T(8,128)(2,1)S(1)}, bf16[2,48,1536]{2,1,0:T(8,128)(2,1)S(1)}, u32[]{:S(2)}, u32[]{:S(2)}) collective-permute-start(bf16[2,48,1536]{2,1,0:T(8,128)(2,1)S(1)} %pad_maximum_fusion.12), channel_id=1, source_target_pairs={{0,16},{1,17},{2,18},{3,19},{4,20},{5,21},{6,22},{7,23},{8,24},{9,... | collective-permute-start | bytes 884744 | tf_op jit(solution)/shard_map/ppermute | solution.py:53
  40.9 20.8 %collective-permute-start.9 = (bf16[2,4,48,768]{3,2,1,0:T(8,128)(2,1)}, bf16[2,4,48,768]{3,2,1,0:T(8,128)(2,1)}, u32[]{:S(2)}, u32[]{:S(2)}) collective-permute-start(bf16[2,4,48,768]{3,2,1,0:T(8,128)(2,1)} %pad_maximum_fusion.6.refs_3_.refs_10_), channel_id=1, source_target_pairs={{0,2},{1,3},{2,0},{3,1},{4,6},{5,7},{6,4},{7,5},{8,10},{9,11},{10,... | collective-permute-start | bytes 1769480 | tf_op jit(solution)/shard_map/ppermute | solution.py:53
  54.6 17.7 %collective-permute-start.16 = (bf16[4,48,1536]{2,1,0:T(8,128)(2,1)}, bf16[4,48,1536]{2,1,0:T(8,128)(2,1)}, u32[]{:S(2)}, u32[]{:S(2)}) collective-permute-start(bf16[4,48,1536]{2,1,0:T(8,128)(2,1)} %get-tuple-element.259), channel_id=1, source_target_pairs={{0,4},{1,5},{2,6},{3,7},{4,0},{5,1},{6,2},{7,3},{8,12},{9,13},{10,... | collective-permute-start | bytes 1769480 | tf_op jit(solution)/shard_map/ppermute | solution.py:53
  55.1 17.2 %collective-permute-start.13 = (bf16[2,4,48,768]{3,2,1,0:T(8,128)(2,1)S(1)}, bf16[2,4,48,768]{3,2,1,0:T(8,128)(2,1)}, u32[]{:S(2)}, u32[]{:S(2)}) collective-permute-start(bf16[2,4,48,768]{3,2,1,0:T(8,128)(2,1)S(1)} %collective-permute-done.10.refs_5_.refs_12_), channel_id=1, source_target_pairs={{0,2},{1,3},{2,0},{3,1},{4,6},{5,7},{6,4},{7,5},{8,10},{9,11},{10,... | collective-permute-start | bytes 1769480 | tf_op jit(solution)/shard_map/ppermute | solution.py:53
  55.2 17.2 %collective-permute-start.15 = (bf16[2,4,48,768]{3,2,1,0:T(8,128)(2,1)S(1)}, bf16[2,4,48,768]{3,2,1,0:T(8,128)(2,1)S(1)}, u32[]{:S(2)}, u32[]{:S(2)}) collective-permute-start(bf16[2,4,48,768]{3,2,1,0:T(8,128)(2,1)S(1)} %collective-permute-done.11.refs_9_.refs_11_.refs_16_), channel_id=1, source_target_pairs={{0,2},{1,3},{2,0},{3,1},{4,6},{5,7},{6,4},{7,5},{8,10},{9,11},{10,... | collective-permute-start | bytes 1769480 | tf_op jit(solution)/shard_map/ppermute | solution.py:53
  56.7 23.8 %all-to-all-start = ((bf16[16,32,768]{2,1,0:T(8,128)(2,1)}), bf16[16,32,768]{2,1,0:T(8,128)(2,1)S(1)}, u32[]{:S(2)}, u32[]{:S(2)}) async-start(bf16[16,32,768]{2,1,0:T(8,128)(2,1)} %bitcast.95), calls=%async_computation | async-start | bytes 1572864 | tf_op jit(solution)/shard_map/all_to_all | solution.py:809
  75.0 33.3 %collective-permute-start.19 = (bf16[2,4,48,1536]{3,2,1,0:T(8,128)(2,1)}, bf16[2,4,48,1536]{3,2,1,0:T(8,128)(2,1)}, u32[]{:S(2)}, u32[]{:S(2)}) collective-permute-start(bf16[2,4,48,1536]{3,2,1,0:T(8,128)(2,1)} %pad_maximum_fusion.1.refs_9_), channel_id=1, source_target_pairs={{0,4},{1,5},{2,6},{3,7},{4,0},{5,1},{6,2},{7,3},{8,12},{9,13},{10,... | collective-permute-start | bytes 3538952 | tf_op jit(solution)/shard_map/ppermute | solution.py:53
  75.0 33.3 %collective-permute-start.21 = (bf16[2,4,48,1536]{3,2,1,0:T(8,128)(2,1)}, bf16[2,4,48,1536]{3,2,1,0:T(8,128)(2,1)}, u32[]{:S(2)}, u32[]{:S(2)}) collective-permute-start(bf16[2,4,48,1536]{3,2,1,0:T(8,128)(2,1)} %pad_maximum_fusion.1.refs_9_), channel_id=1, source_target_pairs={{0,2},{1,3},{2,0},{3,1},{4,6},{5,7},{6,4},{7,5},{8,10},{9,11},{10,... | collective-permute-start | bytes 3538952 | tf_op jit(solution)/shard_map/ppermute | solution.py:53
  76.2 36.2 %collective-permute-start.18 = (bf16[2,4,48,1536]{3,2,1,0:T(8,128)(2,1)S(1)}, bf16[2,4,48,1536]{3,2,1,0:T(8,128)(2,1)S(1)}, u32[]{:S(2)}, u32[]{:S(2)}) collective-permute-start(bf16[2,4,48,1536]{3,2,1,0:T(8,128)(2,1)S(1)} %pad_maximum_fusion.refs_5_), channel_id=1, source_target_pairs={{0,1},{1,0},{2,3},{3,2},{4,5},{5,4},{6,7},{7,6},{8,9},{9,8},{10,11... | collective-permute-start | bytes 3538952 | tf_op jit(solution)/shard_map/ppermute | solution.py:53
  77.8 34.6 %collective-permute-start.20 = (bf16[2,4,48,1536]{3,2,1,0:T(8,128)(2,1)S(1)}, bf16[2,4,48,1536]{3,2,1,0:T(8,128)(2,1)}, u32[]{:S(2)}, u32[]{:S(2)}) collective-permute-start(bf16[2,4,48,1536]{3,2,1,0:T(8,128)(2,1)S(1)} %pad_maximum_fusion.refs_5_), channel_id=1, source_target_pairs={{0,2},{1,3},{2,0},{3,1},{4,6},{5,7},{6,4},{7,5},{8,10},{9,11},{10,... | collective-permute-start | bytes 3538952 | tf_op jit(solution)/shard_map/ppermute | solution.py:53
  82.1 35.2 %all-to-all-start.1 = ((bf16[32,16,768]{2,1,0:T(8,128)(2,1)}), bf16[32,16,768]{2,1,0:T(8,128)(2,1)}, u32[]{:S(2)}, u32[]{:S(2)}) async-start(bf16[32,16,768]{2,1,0:T(8,128)(2,1)} %pick.2), calls=%async_computation.1 | async-start | bytes 1572864 | tf_op jit(solution)/shard_map/all_to_all | solution.py:818
  140.8 45.4 %all-to-all-start.2 = ((bf16[32,16,768]{2,1,0:T(8,128)(2,1)}), bf16[32,16,768]{2,1,0:T(8,128)(2,1)S(1)}, u32[]{:S(2)}, u32[]{:S(2)}) async-start(bf16[32,16,768]{2,1,0:T(8,128)(2,1)} %bitcast.100), calls=%async_computation.2 | async-start | bytes 1572864 | tf_op jit(solution)/shard_map/all_to_all | solution.py:825
  152.4 33.9 %collective-permute-start.25 = (bf16[2,4,48,1536]{3,2,1,0:T(8,128)(2,1)}, bf16[2,4,48,1536]{3,2,1,0:T(8,128)(2,1)}, u32[]{:S(2)}, u32[]{:S(2)}) collective-permute-start(bf16[2,4,48,1536]{3,2,1,0:T(8,128)(2,1)} %get-tuple-element.195), channel_id=1, source_target_pairs={{0,4},{1,5},{2,6},{3,7},{4,0},{5,1},{6,2},{7,3},{8,12},{9,13},{10,... | collective-permute-start | bytes 3538952 | tf_op jit(solution)/shard_map/ppermute | solution.py:53
  154.5 31.8 %collective-permute-start.26 = (bf16[2,4,48,1536]{3,2,1,0:T(8,128)(2,1)}, bf16[2,4,48,1536]{3,2,1,0:T(8,128)(2,1)}, u32[]{:S(2)}, u32[]{:S(2)}) collective-permute-start(bf16[2,4,48,1536]{3,2,1,0:T(8,128)(2,1)} %get-tuple-element.196), channel_id=1, source_target_pairs={{0,1},{1,0},{2,3},{3,2},{4,5},{5,4},{6,7},{7,6},{8,9},{9,8},{10,11... | collective-permute-start | bytes 3538952 | tf_op jit(solution)/shard_map/ppermute | solution.py:53
  189.9 15.6 %collective-permute-start.29 = (bf16[2,2,48,1536]{3,2,1,0:T(8,128)(2,1)}, bf16[2,2,48,1536]{3,2,1,0:T(8,128)(2,1)}, u32[]{:S(2)}, u32[]{:S(2)}) collective-permute-start(bf16[2,2,48,1536]{3,2,1,0:T(8,128)(2,1)} %get-tuple-element.203), channel_id=1, source_target_pairs={{0,1},{1,0},{2,3},{3,2},{4,5},{5,4},{6,7},{7,6},{8,9},{9,8},{10,11... | collective-permute-start | bytes 1769480 | tf_op jit(solution)/shard_map/ppermute | solution.py:53
  190.5 20.7 %collective-permute-start.30 = (bf16[2,2,48,1536]{3,2,1,0:T(8,128)(2,1)}, bf16[2,2,48,1536]{3,2,1,0:T(8,128)(2,1)}, u32[]{:S(2)}, u32[]{:S(2)}) collective-permute-start(bf16[2,2,48,1536]{3,2,1,0:T(8,128)(2,1)} %get-tuple-element.204), channel_id=1, source_target_pairs={{0,4},{1,5},{2,6},{3,7},{4,0},{5,1},{6,2},{7,3},{8,12},{9,13},{10,... | collective-permute-start | bytes 1769480 | tf_op jit(solution)/shard_map/ppermute | solution.py:53
  192.3 38.7 %all-to-all-start.3 = ((bf16[16,32,768]{2,1,0:T(8,128)(2,1)}), bf16[16,32,768]{2,1,0:T(8,128)(2,1)}, u32[]{:S(2)}, u32[]{:S(2)}) async-start(bf16[16,32,768]{2,1,0:T(8,128)(2,1)} %bitcast.34), calls=%async_computation.3 | async-start | bytes 1572864 | tf_op jit(solution)/shard_map/all_to_all | solution.py:835
  211.2 29.0 %collective-permute-start.31 = (bf16[208,1536]{1,0:T(8,128)(2,1)}, bf16[208,1536]{1,0:T(8,128)(2,1)S(1)}, u32[]{:S(2)}, u32[]{:S(2)}) collective-permute-start(bf16[208,1536]{1,0:T(8,128)(2,1)} %get-tuple-element.205), channel_id=1, source_target_pairs={{0,1},{1,0},{2,3},{3,2},{4,5},{5,4},{6,7},{7,6},{8,9},{9,8},{10,11... | collective-permute-start | bytes 1916936 | tf_op jit(solution)/shard_map/ppermute | solution.py:53
  212.7 27.5 %collective-permute-start.32 = (bf16[208,1536]{1,0:T(8,128)(2,1)S(1)}, bf16[208,1536]{1,0:T(8,128)(2,1)S(1)}, u32[]{:S(2)}, u32[]{:S(2)}) collective-permute-start(bf16[208,1536]{1,0:T(8,128)(2,1)S(1)} %get-tuple-element.206), channel_id=1, source_target_pairs={{0,4},{1,5},{2,6},{3,7},{4,0},{5,1},{6,2},{7,3},{8,12},{9,13},{10,... | collective-permute-start | bytes 1916936 | tf_op jit(solution)/shard_map/ppermute | solution.py:53
  212.7 29.7 %collective-permute-start.33 = (bf16[208,1536]{1,0:T(8,128)(2,1)S(1)}, bf16[208,1536]{1,0:T(8,128)(2,1)S(1)}, u32[]{:S(2)}, u32[]{:S(2)}) collective-permute-start(bf16[208,1536]{1,0:T(8,128)(2,1)S(1)} %get-tuple-element.207), channel_id=1, source_target_pairs={{0,5},{1,4},{2,7},{3,6},{4,1},{5,0},{6,3},{7,2},{8,13},{9,12},{10,... | collective-permute-start | bytes 1916936 | tf_op jit(solution)/shard_map/ppermute | solution.py:53
  217.8 22.4 %collective-permute-start.35 = (bf16[2,48,1536]{2,1,0:T(8,128)(2,1)}, bf16[2,48,1536]{2,1,0:T(8,128)(2,1)}, u32[]{:S(2)}, u32[]{:S(2)}) collective-permute-start(bf16[2,48,1536]{2,1,0:T(8,128)(2,1)} %get-tuple-element.211), channel_id=1, source_target_pairs={{0,16},{1,17},{2,18},{3,19},{4,20},{5,21},{6,22},{7,23},{8,24},{9,... | collective-permute-start | bytes 884744 | tf_op jit(solution)/shard_map/ppermute | solution.py:53
  249.1 15.1 %collective-permute-start.39 = (bf16[64,1536]{1,0:T(8,128)(2,1)S(1)}, bf16[64,1536]{1,0:T(8,128)(2,1)S(1)}, u32[]{:S(2)}, u32[]{:S(2)}) collective-permute-start(bf16[64,1536]{1,0:T(8,128)(2,1)S(1)} %get-tuple-element.227), channel_id=1, source_target_pairs={{0,16},{1,17},{2,18},{3,19},{4,20},{5,21},{6,22},{7,23},{8,24},{9,... | collective-permute-start | bytes 589832 | tf_op jit(solution)/shard_map/ppermute | solution.py:53
  249.3 14.9 %collective-permute-start.40 = (bf16[64,1536]{1,0:T(8,128)(2,1)S(1)}, bf16[64,1536]{1,0:T(8,128)(2,1)S(1)}, u32[]{:S(2)}, u32[]{:S(2)}) collective-permute-start(bf16[64,1536]{1,0:T(8,128)(2,1)S(1)} %get-tuple-element.228), channel_id=1, source_target_pairs={{0,24},{1,25},{2,26},{3,27},{4,28},{5,29},{6,30},{7,31},{8,16},{9,... | collective-permute-start | bytes 589832 | tf_op jit(solution)/shard_map/ppermute | solution.py:53
  (50 other events, 437.6 us)

commit v3 on v2

--- a/solution.py
+++ b/solution.py
@@ -293,6 +293,16 @@
         def _(t):
             here = pl.ds(pl.multiple_of(t * TILE, TILE), TILE)
             store(scalars, grads, 1, t, dot_tn(gffn[...], act[:, here]).astype(BF16))
+
+        if len(grad_outs) == 2:
+            far = n ^ scalars[AT_Y]
+            sent += [move(grads.at[c, 1, far], o.at[1, far]) for c, o in enumerate(grad_outs)]
+
+    for n in range(2):
+
+        @pl.loop(n * tiles // 2, (n + 1) * tiles // 2)
+        def _(t):
+            here = pl.ds(pl.multiple_of(t * TILE, TILE), TILE)
             g = (dot_nn(gffn[...], down[:, here]) * slope[:, here].astype(F32)).astype(BF16)
             slope[:, here] = g
             unit_sums[0:1, here] = column_sum(g.astype(F32))
@@ -302,8 +312,7 @@
         sent.append(move(slope.at[:, done], ghid_out.at[:, done]))
         if len(grad_outs) == 2:
             far = n ^ scalars[AT_Y]
-            for c, o in enumerate(grad_outs):
-                sent += [move(grads.at[c, 0, :, far], o.at[0, :, far]), move(grads.at[c, 1, far], o.at[1, far])]
+            sent += [move(grads.at[c, 0, :, far], o.at[0, :, far]) for c, o in enumerate(grad_outs)]
     if len(grad_outs) == 1:
         sent.append(move(grads.at[0], grad_outs[0]))
     wait(sent)
@@ -313,12 +322,21 @@
     weights, head_weights, _, (first, gattn, gatt, sums), scratch = refs
     move = Mover(scratch[-1])
     ghid, normal, rscale, acc, w_up, w_out = scratch[:-1]
-    early = [move(ghid_in, ghid)] + load(move, scalars, weights, w_up)
+    half = ghid.shape[1] // 2
+    parts = [pl.ds(pl.multiple_of((scalars[AT_Y] ^ n) * half, 128), half) for n in range(2)]
+    mine, others = ([move(ghid_in.at[:, at], ghid.at[:, at])] for at in parts)
+    copies = load(move, scalars, weights, w_up)
+    cut = max(len(copies) // 2, 1)
+    mine += copies[:cut]
+    others += copies[cut:]
     late = [move(s, d) for s, d in ((normal_in, normal), (rscale_in, rscale))]
     last = load_out(move, scalars, head_weights, w_out)
     seq, features = second.shape
-    wait(early)
-    acc[...] = dot_nt(ghid[...], flat(w_up)[...])
+    up = flat(w_up)
+    wait(mine)
+    acc[...] = dot_nt(ghid[:, parts[0]], up[:, parts[0]])
+    wait(others)
+    acc[...] += dot_nt(ghid[:, parts[1]], up[:, parts[1]])
     wait(late)
     sums[...] = jnp.zeros_like(sums)
 

time: 268 us -> 268 us (level)
  transfers between devices with their start and end apart: 45 -> 45, of which waited for: 21 -> 22; matrix products, arithmetic and copies ran while one was open for 8% -> 8% of each run, Pallas kernels for 22% -> 22%
where the time goes in v3:
time: 268 us; the launch traced here: 266 us
  waiting for transfers between devices  89.8 us (34%)
  Pallas kernels  83.5 us (31%)
  starting transfers between devices  68.1 us (25%)
  other arithmetic  15.6 us (6%)
  local copies, waits for them, and re-layouts  7 us (3%)
    ppermute x41, waiting for transfers between devices, exchange(): return lax.ppermute(value, BOTH, [(i, i ^ mask) for i in range(count)])  88.7 us
    pallas_call x4, Pallas kernels, run(): pl.pallas_call(body, out_shape=(*(pltpu.HBM(o.shape, o.dtype) for o in ou...  67.2 us
    ppermute x41, starting transfers between devices, exchange(): return lax.ppermute(value, BOTH, [(i, i ^ mask) for i in range(count)])  45.6 us
    pallas_call x2, Pallas kernels, combine(): pl.pallas_call(functools.partial(combine_kernel, jobs), out_shape=[pltpu....  6.38 us
    all_to_all x1, starting transfers between devices, collect_start(): return lax.all_to_all(pieces, BOTH, split_axis=0, concat_axis=0, tiled=True)  6.03 us
    all_to_all x1, starting transfers between devices, deal_finish(): got = lax.all_to_all(chosen, BOTH, split_axis=0, concat_axis=0, tiled=True)  5.76 us
    all_to_all x1, starting transfers between devices, collect_start_back(): return lax.all_to_all(chosen, 'dp', split_axis=0, concat_axis=0, tiled=True)  5.65 us
  transfers between devices with their start and end apart: 45, of which 22 were waited for; matrix products, arithmetic and copies ran while one was open for 8% of the time, Pallas kernels for 22%

profile of v3, /device:TPU:0, one launch (start us, length us, event | category | flops | bytes accessed | tf_op | source)
XLA Modules:
  0.0 265.6 jit_solution(6980688713322672780)
XLA Ops:
  10.6 3.6 %collective-permute-done.4 = f32[6,384]{1,0:T(8,128)S(1)} collective-permute-done((f32[6,384]{1,0:T(8,128)S(1)}, f32[6,384]{1,0:T(8,128)S(1)}, u32[]{:S(2)}, u32[]{:S(2)}) %collective-permute-start.4) | collective-permute-done | bytes 9248 | tf_op jit(solution)/shard_map/ppermute | solution.py:53
  24.3 4.7 %collective-permute-done.7 = bf16[2,48,1536]{2,1,0:T(8,128)(2,1)S(1)} collective-permute-done((bf16[2,48,1536]{2,1,0:T(8,128)(2,1)S(1)}, bf16[2,48,1536]{2,1,0:T(8,128)(2,1)S(1)}, u32[]{:S(2)}, u32[]{:S(2)}) %collective-permute-start.7) | collective-permute-done | bytes 294944 | tf_op jit(solution)/shard_map/ppermute | solution.py:53
  28.9 6.5 %collective-permute-done.8 = bf16[2,48,1536]{2,1,0:T(8,128)(2,1)S(1)} collective-permute-done((bf16[2,48,1536]{2,1,0:T(8,128)(2,1)S(1)}, bf16[2,48,1536]{2,1,0:T(8,128)(2,1)S(1)}, u32[]{:S(2)}, u32[]{:S(2)}) %collective-permute-start.8) | collective-permute-done | bytes 294944 | tf_op jit(solution)/shard_map/ppermute | solution.py:53
  41.4 5.8 %collective-permute-done.12 = bf16[2,48,1536]{2,1,0:T(8,128)(2,1)S(1)} collective-permute-done((bf16[2,48,1536]{2,1,0:T(8,128)(2,1)S(1)}, bf16[2,48,1536]{2,1,0:T(8,128)(2,1)S(1)}, u32[]{:S(2)}, u32[]{:S(2)}) %collective-permute-start.12) | collective-permute-done | bytes 294944 | tf_op jit(solution)/shard_map/ppermute | solution.py:53
  56.7 5.0 %all-to-all-start = ((bf16[16,32,768]{2,1,0:T(8,128)(2,1)}), bf16[16,32,768]{2,1,0:T(8,128)(2,1)S(1)}, u32[]{:S(2)}, u32[]{:S(2)}) async-start(bf16[16,32,768]{2,1,0:T(8,128)(2,1)} %bitcast.95), calls=%async_computation | async-start | bytes 1572864 | tf_op jit(solution)/shard_map/all_to_all | solution.py:827
  61.7 4.1 %collective-permute-done.17 = bf16[4,48,1536]{2,1,0:T(8,128)(2,1)} collective-permute-done((bf16[4,48,1536]{2,1,0:T(8,128)(2,1)}, bf16[4,48,1536]{2,1,0:T(8,128)(2,1)}, u32[]{:S(2)}, u32[]{:S(2)}) %collective-permute-start.17) | collective-permute-done | bytes 589856 | tf_op jit(solution)/shard_map/ppermute | solution.py:53
  65.8 6.5 %collective-permute-done.16 = bf16[4,48,1536]{2,1,0:T(8,128)(2,1)} collective-permute-done((bf16[4,48,1536]{2,1,0:T(8,128)(2,1)}, bf16[4,48,1536]{2,1,0:T(8,128)(2,1)}, u32[]{:S(2)}, u32[]{:S(2)}) %collective-permute-start.16) | collective-permute-done | bytes 589856 | tf_op jit(solution)/shard_map/ppermute | solution.py:53
  82.1 5.8 %all-to-all-start.1 = ((bf16[32,16,768]{2,1,0:T(8,128)(2,1)}), bf16[32,16,768]{2,1,0:T(8,128)(2,1)}, u32[]{:S(2)}, u32[]{:S(2)}) async-start(bf16[32,16,768]{2,1,0:T(8,128)(2,1)} %pick.2), calls=%async_computation.1 | async-start | bytes 1572864 | tf_op jit(solution)/shard_map/all_to_all | solution.py:836
  88.1 15.6 %attend.1 = (bf16[512,768]{1,0:T(8,128)(2,1)}, bf16[512,768]{1,0:T(8,128)(2,1)}, bf16[512,768]{1,0:T(8,128)(2,1)}, bf16[512,768]{1,0:T(8,128)(2,1)}, f32[512,128...) custom-call(s32[5]{0:T(128)S(1)} %stack.129.scalars, ...), custom_call_target="tpu_custom_call" | custom-call | flops 300000000 | bytes 900000 | tf_op jit(solution)/shard_map/attend/pallas_call | solution.py:520
  103.6 4.6 %collective-permute-done.19.refs_11_ = bf16[2,4,48,1536]{3,2,1,0:T(8,128)(2,1)} collective-permute-done((bf16[2,4,48,1536]{3,2,1,0:T(8,128)(2,1)}, bf16[2,4,48,1536]{3,2,1,0:T(8,128)(2,1)}, u32[]{:S(2)}, u32[]{:S(2)}) %collective-permute-start.19) | collective-permute-done | bytes 1179680 | tf_op jit(solution)/shard_map/ppermute | solution.py:53
  108.2 4.2 %collective-permute-done.18.refs_7_ = bf16[2,4,48,1536]{3,2,1,0:T(8,128)(2,1)S(1)} collective-permute-done((bf16[2,4,48,1536]{3,2,1,0:T(8,128)(2,1)S(1)}, bf16[2,4,48,1536]{3,2,1,0:T(8,128)(2,1)S(1)}, u32[]{:S(2)}, u32[]{:S(2)}) %collective-permute-start.18) | collective-permute-done | bytes 1179680 | tf_op jit(solution)/shard_map/ppermute | solution.py:53
  117.3 23.3 %middle.1 = (bf16[16,2,16,768]{3,2,1,0:T(8,128)(2,1)}, bf16[512,3072]{1,0:T(8,128)(2,1)}, bf16[2,2,2,4,48,1536]{5,4,3,2,1,0:T(8,128)(2,1)}, bf16[2,2,2,4,48,1536...) custom-call(s32[5]{0:T(128)S(1)} %stack.129.scalars, ...), custom_call_target="tpu_custom_call" | custom-call | flops 480000000 | bytes 1440000 | tf_op jit(solution)/shard_map/middle/pallas_call | solution.py:520
  140.8 6.0 %all-to-all-start.2 = ((bf16[32,16,768]{2,1,0:T(8,128)(2,1)}), bf16[32,16,768]{2,1,0:T(8,128)(2,1)S(1)}, u32[]{:S(2)}, u32[]{:S(2)}) async-start(bf16[32,16,768]{2,1,0:T(8,128)(2,1)} %bitcast.100), calls=%async_computation.2 | async-start | bytes 1572864 | tf_op jit(solution)/shard_map/all_to_all | solution.py:843
  148.9 3.5 %first_side.1 = (bf16[2,4,48,1536]{3,2,1,0:T(8,128)(2,1)}, bf16[2,4,48,1536]{3,2,1,0:T(8,128)(2,1)}) custom-call(bf16[2,2,2,4,48,1536]{5,4,3,2,1,0:T(8,128)(2,1)} %get-tuple-element.193.refs_0_.keep, bf16[2,2,2,4,48,1536]{5,4,3,2,1,0:T(8,128)(2,1)} %collective-permute-done.24.refs_1_.near), custom_call_target="tpu_custom_call" | custom-call | flops 60000000 | bytes 180000 | tf_op jit(solution)/shard_map/first_side/pallas_call | solution.py:726
  157.3 9.4 %normed.1 = (f32[512,768]{1,0:T(8,128)S(1)}, bf16[512,768]{1,0:T(8,128)(2,1)S(1)}, bf16[512,768]{1,0:T(8,128)(2,1)S(1)}, f32[3,768]{1,0:T(4,128)S(1)}) custom-call(s32[5]{0:T(128)S(1)} %stack.129.scalars, bf16[512,3072]{1,0:T(8,128)(2,1)} %get-tuple-element.175.refs_0_, f32[512,768]{1,0:T(8,128)S(1)} %get-tuple-element.176.refs_1_, ...), custom_call_target="tpu_custom_call" | custom-call | flops 160000000 | bytes 480000 | tf_op jit(solution)/shard_map/normed/pallas_call | solution.py:520
  166.7 18.9 %last.1 = (bf16[256,768]{1,0:T(8,128)(2,1)}, bf16[256,768]{1,0:T(8,128)(2,1)}, bf16[4,4,48,1536]{3,2,1,0:T(8,128)(2,1)}, bf16[4,4,48,1536]{3,2,1,0:T(8,128)(2,1)}, f32[2,768]{1,0:T(2,128)S(1)}) custom-call(s32[5]{0:T(128)S(1)} %stack.129.scalars, bf16[512,768]{1,0:T(8,128)(2,1)S(1)} %get-tuple-element.178.refs_0_, ...), custom_call_target="tpu_custom_call" | custom-call | flops 400000000 | bytes 1200000 | tf_op jit(solution)/shard_map/last/pallas_call | solution.py:520
  192.3 5.7 %all-to-all-start.3 = ((bf16[16,32,768]{2,1,0:T(8,128)(2,1)}), bf16[16,32,768]{2,1,0:T(8,128)(2,1)}, u32[]{:S(2)}, u32[]{:S(2)}) async-start(bf16[16,32,768]{2,1,0:T(8,128)(2,1)} %bitcast.34), calls=%async_computation.3 | async-start | bytes 1572864 | tf_op jit(solution)/shard_map/all_to_all | solution.py:853
  201.1 4.0 %collective-permute-done.29 = bf16[2,2,48,1536]{3,2,1,0:T(8,128)(2,1)} collective-permute-done((bf16[2,2,48,1536]{3,2,1,0:T(8,128)(2,1)}, bf16[2,2,48,1536]{3,2,1,0:T(8,128)(2,1)}, u32[]{:S(2)}, u32[]{:S(2)}) %collective-permute-start.29) | collective-permute-done | bytes 589856 | tf_op jit(solution)/shard_map/ppermute | solution.py:53
  205.0 6.3 %collective-permute-done.30 = bf16[2,2,48,1536]{3,2,1,0:T(8,128)(2,1)} collective-permute-done((bf16[2,2,48,1536]{3,2,1,0:T(8,128)(2,1)}, bf16[2,2,48,1536]{3,2,1,0:T(8,128)(2,1)}, u32[]{:S(2)}, u32[]{:S(2)}) %collective-permute-start.30) | collective-permute-done | bytes 589856 | tf_op jit(solution)/shard_map/ppermute | solution.py:53
  217.9 3.6 %collective-permute-start.35 = (bf16[2,48,1536]{2,1,0:T(8,128)(2,1)}, bf16[2,48,1536]{2,1,0:T(8,128)(2,1)}, u32[]{:S(2)}, u32[]{:S(2)}) collective-permute-start(bf16[2,48,1536]{2,1,0:T(8,128)(2,1)} %get-tuple-element.211), channel_id=1, source_target_pairs={{0,16},{1,17},{2,18},{3,19},{4,20},{5,21},{6,22},{7,23},{8,24},{9,... | collective-permute-start | bytes 884744 | tf_op jit(solution)/shard_map/ppermute | solution.py:53
  221.6 7.1 %collective-permute-done.34 = bf16[2,48,1536]{2,1,0:T(8,128)(2,1)S(1)} collective-permute-done((bf16[2,48,1536]{2,1,0:T(8,128)(2,1)}, bf16[2,48,1536]{2,1,0:T(8,128)(2,1)S(1)}, u32[]{:S(2)}, u32[]{:S(2)}) %collective-permute-start.34) | collective-permute-done | bytes 294944 | tf_op jit(solution)/shard_map/ppermute | solution.py:53
  231.1 8.9 %collective-permute-done.35 = bf16[2,48,1536]{2,1,0:T(8,128)(2,1)} collective-permute-done((bf16[2,48,1536]{2,1,0:T(8,128)(2,1)}, bf16[2,48,1536]{2,1,0:T(8,128)(2,1)}, u32[]{:S(2)}, u32[]{:S(2)}) %collective-permute-start.35) | collective-permute-done | bytes 294944 | tf_op jit(solution)/shard_map/ppermute | solution.py:53
  245.3 3.4 %collective-permute-start.37 = (bf16[64,1536]{1,0:T(8,128)(2,1)S(1)}, bf16[64,1536]{1,0:T(8,128)(2,1)S(1)}, u32[]{:S(2)}, u32[]{:S(2)}) collective-permute-start(bf16[64,1536]{1,0:T(8,128)(2,1)S(1)} %get-tuple-element.220), channel_id=1, source_target_pairs={{0,8},{1,9},{2,10},{3,11},{4,12},{5,13},{6,14},{7,15},{8,0},{9,1},... | collective-permute-start | bytes 589832 | tf_op jit(solution)/shard_map/ppermute | solution.py:53
  256.9 7.1 %collective-permute-done.39.second = bf16[64,1536]{1,0:T(8,128)(2,1)S(1)} collective-permute-done((bf16[64,1536]{1,0:T(8,128)(2,1)S(1)}, bf16[64,1536]{1,0:T(8,128)(2,1)S(1)}, u32[]{:S(2)}, u32[]{:S(2)}) %collective-permute-start.39) | collective-permute-done | bytes 196640 | tf_op jit(solution)/shard_map/ppermute | solution.py:53
  (192 shorter events, 90.5 us)
Async XLA Ops:
  1.8 19.5 %collective-permute-start.3 = (bf16[256,768]{1,0:T(8,128)(2,1)S(1)}, bf16[256,768]{1,0:T(8,128)(2,1)S(1)}, u32[]{:S(2)}, u32[]{:S(2)}) collective-permute-start(bf16[256,768]{1,0:T(8,128)(2,1)S(1)} %dynamic-slice_bitcast_fusion), channel_id=1, source_target_pairs={{0,1},{1,0},{2,3},{3,2},{4,5},{5,4},{6,7},{7,6},{8,9},{9,8},{10,11... | collective-permute-start | bytes 1179656 | tf_op jit(solution)/shard_map/ppermute | solution.py:53
  16.0 19.4 %collective-permute-start.8 = (bf16[2,48,1536]{2,1,0:T(8,128)(2,1)S(1)}, bf16[2,48,1536]{2,1,0:T(8,128)(2,1)S(1)}, u32[]{:S(2)}, u32[]{:S(2)}) collective-permute-start(bf16[2,48,1536]{2,1,0:T(8,128)(2,1)S(1)} %pad_maximum_fusion.12), channel_id=1, source_target_pairs={{0,16},{1,17},{2,18},{3,19},{4,20},{5,21},{6,22},{7,23},{8,24},{9,... | collective-permute-start | bytes 884744 | tf_op jit(solution)/shard_map/ppermute | solution.py:53
  40.9 20.8 %collective-permute-start.9 = (bf16[2,4,48,768]{3,2,1,0:T(8,128)(2,1)}, bf16[2,4,48,768]{3,2,1,0:T(8,128)(2,1)}, u32[]{:S(2)}, u32[]{:S(2)}) collective-permute-start(bf16[2,4,48,768]{3,2,1,0:T(8,128)(2,1)} %pad_maximum_fusion.6.refs_3_.refs_10_), channel_id=1, source_target_pairs={{0,2},{1,3},{2,0},{3,1},{4,6},{5,7},{6,4},{7,5},{8,10},{9,11},{10,... | collective-permute-start | bytes 1769480 | tf_op jit(solution)/shard_map/ppermute | solution.py:53
  54.6 17.7 %collective-permute-start.16 = (bf16[4,48,1536]{2,1,0:T(8,128)(2,1)}, bf16[4,48,1536]{2,1,0:T(8,128)(2,1)}, u32[]{:S(2)}, u32[]{:S(2)}) collective-permute-start(bf16[4,48,1536]{2,1,0:T(8,128)(2,1)} %get-tuple-element.259), channel_id=1, source_target_pairs={{0,4},{1,5},{2,6},{3,7},{4,0},{5,1},{6,2},{7,3},{8,12},{9,13},{10,... | collective-permute-start | bytes 1769480 | tf_op jit(solution)/shard_map/ppermute | solution.py:53
  55.1 17.2 %collective-permute-start.13 = (bf16[2,4,48,768]{3,2,1,0:T(8,128)(2,1)S(1)}, bf16[2,4,48,768]{3,2,1,0:T(8,128)(2,1)}, u32[]{:S(2)}, u32[]{:S(2)}) collective-permute-start(bf16[2,4,48,768]{3,2,1,0:T(8,128)(2,1)S(1)} %collective-permute-done.10.refs_5_.refs_12_), channel_id=1, source_target_pairs={{0,2},{1,3},{2,0},{3,1},{4,6},{5,7},{6,4},{7,5},{8,10},{9,11},{10,... | collective-permute-start | bytes 1769480 | tf_op jit(solution)/shard_map/ppermute | solution.py:53
  55.2 17.2 %collective-permute-start.15 = (bf16[2,4,48,768]{3,2,1,0:T(8,128)(2,1)S(1)}, bf16[2,4,48,768]{3,2,1,0:T(8,128)(2,1)S(1)}, u32[]{:S(2)}, u32[]{:S(2)}) collective-permute-start(bf16[2,4,48,768]{3,2,1,0:T(8,128)(2,1)S(1)} %collective-permute-done.11.refs_9_.refs_11_.refs_16_), channel_id=1, source_target_pairs={{0,2},{1,3},{2,0},{3,1},{4,6},{5,7},{6,4},{7,5},{8,10},{9,11},{10,... | collective-permute-start | bytes 1769480 | tf_op jit(solution)/shard_map/ppermute | solution.py:53
  56.7 23.8 %all-to-all-start = ((bf16[16,32,768]{2,1,0:T(8,128)(2,1)}), bf16[16,32,768]{2,1,0:T(8,128)(2,1)S(1)}, u32[]{:S(2)}, u32[]{:S(2)}) async-start(bf16[16,32,768]{2,1,0:T(8,128)(2,1)} %bitcast.95), calls=%async_computation | async-start | bytes 1572864 | tf_op jit(solution)/shard_map/all_to_all | solution.py:827
  75.0 33.3 %collective-permute-start.19 = (bf16[2,4,48,1536]{3,2,1,0:T(8,128)(2,1)}, bf16[2,4,48,1536]{3,2,1,0:T(8,128)(2,1)}, u32[]{:S(2)}, u32[]{:S(2)}) collective-permute-start(bf16[2,4,48,1536]{3,2,1,0:T(8,128)(2,1)} %pad_maximum_fusion.1.refs_9_), channel_id=1, source_target_pairs={{0,4},{1,5},{2,6},{3,7},{4,0},{5,1},{6,2},{7,3},{8,12},{9,13},{10,... | collective-permute-start | bytes 3538952 | tf_op jit(solution)/shard_map/ppermute | solution.py:53
  75.0 33.3 %collective-permute-start.21 = (bf16[2,4,48,1536]{3,2,1,0:T(8,128)(2,1)}, bf16[2,4,48,1536]{3,2,1,0:T(8,128)(2,1)}, u32[]{:S(2)}, u32[]{:S(2)}) collective-permute-start(bf16[2,4,48,1536]{3,2,1,0:T(8,128)(2,1)} %pad_maximum_fusion.1.refs_9_), channel_id=1, source_target_pairs={{0,2},{1,3},{2,0},{3,1},{4,6},{5,7},{6,4},{7,5},{8,10},{9,11},{10,... | collective-permute-start | bytes 3538952 | tf_op jit(solution)/shard_map/ppermute | solution.py:53
  76.2 36.2 %collective-permute-start.18 = (bf16[2,4,48,1536]{3,2,1,0:T(8,128)(2,1)S(1)}, bf16[2,4,48,1536]{3,2,1,0:T(8,128)(2,1)S(1)}, u32[]{:S(2)}, u32[]{:S(2)}) collective-permute-start(bf16[2,4,48,1536]{3,2,1,0:T(8,128)(2,1)S(1)} %pad_maximum_fusion.refs_5_), channel_id=1, source_target_pairs={{0,1},{1,0},{2,3},{3,2},{4,5},{5,4},{6,7},{7,6},{8,9},{9,8},{10,11... | collective-permute-start | bytes 3538952 | tf_op jit(solution)/shard_map/ppermute | solution.py:53
  77.8 34.6 %collective-permute-start.20 = (bf16[2,4,48,1536]{3,2,1,0:T(8,128)(2,1)S(1)}, bf16[2,4,48,1536]{3,2,1,0:T(8,128)(2,1)}, u32[]{:S(2)}, u32[]{:S(2)}) collective-permute-start(bf16[2,4,48,1536]{3,2,1,0:T(8,128)(2,1)S(1)} %pad_maximum_fusion.refs_5_), channel_id=1, source_target_pairs={{0,2},{1,3},{2,0},{3,1},{4,6},{5,7},{6,4},{7,5},{8,10},{9,11},{10,... | collective-permute-start | bytes 3538952 | tf_op jit(solution)/shard_map/ppermute | solution.py:53
  82.1 35.2 %all-to-all-start.1 = ((bf16[32,16,768]{2,1,0:T(8,128)(2,1)}), bf16[32,16,768]{2,1,0:T(8,128)(2,1)}, u32[]{:S(2)}, u32[]{:S(2)}) async-start(bf16[32,16,768]{2,1,0:T(8,128)(2,1)} %pick.2), calls=%async_computation.1 | async-start | bytes 1572864 | tf_op jit(solution)/shard_map/all_to_all | solution.py:836
  140.8 44.9 %all-to-all-start.2 = ((bf16[32,16,768]{2,1,0:T(8,128)(2,1)}), bf16[32,16,768]{2,1,0:T(8,128)(2,1)S(1)}, u32[]{:S(2)}, u32[]{:S(2)}) async-start(bf16[32,16,768]{2,1,0:T(8,128)(2,1)} %bitcast.100), calls=%async_computation.2 | async-start | bytes 1572864 | tf_op jit(solution)/shard_map/all_to_all | solution.py:843
  152.4 33.3 %collective-permute-start.25 = (bf16[2,4,48,1536]{3,2,1,0:T(8,128)(2,1)}, bf16[2,4,48,1536]{3,2,1,0:T(8,128)(2,1)}, u32[]{:S(2)}, u32[]{:S(2)}) collective-permute-start(bf16[2,4,48,1536]{3,2,1,0:T(8,128)(2,1)} %get-tuple-element.195), channel_id=1, source_target_pairs={{0,4},{1,5},{2,6},{3,7},{4,0},{5,1},{6,2},{7,3},{8,12},{9,13},{10,... | collective-permute-start | bytes 3538952 | tf_op jit(solution)/shard_map/ppermute | solution.py:53
  154.5 31.4 %collective-permute-start.26 = (bf16[2,4,48,1536]{3,2,1,0:T(8,128)(2,1)}, bf16[2,4,48,1536]{3,2,1,0:T(8,128)(2,1)}, u32[]{:S(2)}, u32[]{:S(2)}) collective-permute-start(bf16[2,4,48,1536]{3,2,1,0:T(8,128)(2,1)} %get-tuple-element.196), channel_id=1, source_target_pairs={{0,1},{1,0},{2,3},{3,2},{4,5},{5,4},{6,7},{7,6},{8,9},{9,8},{10,11... | collective-permute-start | bytes 3538952 | tf_op jit(solution)/shard_map/ppermute | solution.py:53
  189.4 15.6 %collective-permute-start.29 = (bf16[2,2,48,1536]{3,2,1,0:T(8,128)(2,1)}, bf16[2,2,48,1536]{3,2,1,0:T(8,128)(2,1)}, u32[]{:S(2)}, u32[]{:S(2)}) collective-permute-start(bf16[2,2,48,1536]{3,2,1,0:T(8,128)(2,1)} %get-tuple-element.203), channel_id=1, source_target_pairs={{0,1},{1,0},{2,3},{3,2},{4,5},{5,4},{6,7},{7,6},{8,9},{9,8},{10,11... | collective-permute-start | bytes 1769480 | tf_op jit(solution)/shard_map/ppermute | solution.py:53
  190.6 20.8 %collective-permute-start.30 = (bf16[2,2,48,1536]{3,2,1,0:T(8,128)(2,1)}, bf16[2,2,48,1536]{3,2,1,0:T(8,128)(2,1)}, u32[]{:S(2)}, u32[]{:S(2)}) collective-permute-start(bf16[2,2,48,1536]{3,2,1,0:T(8,128)(2,1)} %get-tuple-element.204), channel_id=1, source_target_pairs={{0,4},{1,5},{2,6},{3,7},{4,0},{5,1},{6,2},{7,3},{8,12},{9,13},{10,... | collective-permute-start | bytes 1769480 | tf_op jit(solution)/shard_map/ppermute | solution.py:53
  192.3 38.8 %all-to-all-start.3 = ((bf16[16,32,768]{2,1,0:T(8,128)(2,1)}), bf16[16,32,768]{2,1,0:T(8,128)(2,1)}, u32[]{:S(2)}, u32[]{:S(2)}) async-start(bf16[16,32,768]{2,1,0:T(8,128)(2,1)} %bitcast.34), calls=%async_computation.3 | async-start | bytes 1572864 | tf_op jit(solution)/shard_map/all_to_all | solution.py:853
  211.3 28.7 %collective-permute-start.31 = (bf16[208,1536]{1,0:T(8,128)(2,1)}, bf16[208,1536]{1,0:T(8,128)(2,1)S(1)}, u32[]{:S(2)}, u32[]{:S(2)}) collective-permute-start(bf16[208,1536]{1,0:T(8,128)(2,1)} %get-tuple-element.205), channel_id=1, source_target_pairs={{0,1},{1,0},{2,3},{3,2},{4,5},{5,4},{6,7},{7,6},{8,9},{9,8},{10,11... | collective-permute-start | bytes 1916936 | tf_op jit(solution)/shard_map/ppermute | solution.py:53
  211.9 28.2 %collective-permute-start.32 = (bf16[208,1536]{1,0:T(8,128)(2,1)S(1)}, bf16[208,1536]{1,0:T(8,128)(2,1)S(1)}, u32[]{:S(2)}, u32[]{:S(2)}) collective-permute-start(bf16[208,1536]{1,0:T(8,128)(2,1)S(1)} %get-tuple-element.206), channel_id=1, source_target_pairs={{0,4},{1,5},{2,6},{3,7},{4,0},{5,1},{6,2},{7,3},{8,12},{9,13},{10,... | collective-permute-start | bytes 1916936 | tf_op jit(solution)/shard_map/ppermute | solution.py:53
  212.0 29.9 %collective-permute-start.33 = (bf16[208,1536]{1,0:T(8,128)(2,1)S(1)}, bf16[208,1536]{1,0:T(8,128)(2,1)S(1)}, u32[]{:S(2)}, u32[]{:S(2)}) collective-permute-start(bf16[208,1536]{1,0:T(8,128)(2,1)S(1)} %get-tuple-element.207), channel_id=1, source_target_pairs={{0,5},{1,4},{2,7},{3,6},{4,1},{5,0},{6,3},{7,2},{8,13},{9,12},{10,... | collective-permute-start | bytes 1916936 | tf_op jit(solution)/shard_map/ppermute | solution.py:53
  217.9 22.1 %collective-permute-start.35 = (bf16[2,48,1536]{2,1,0:T(8,128)(2,1)}, bf16[2,48,1536]{2,1,0:T(8,128)(2,1)}, u32[]{:S(2)}, u32[]{:S(2)}) collective-permute-start(bf16[2,48,1536]{2,1,0:T(8,128)(2,1)} %get-tuple-element.211), channel_id=1, source_target_pairs={{0,16},{1,17},{2,18},{3,19},{4,20},{5,21},{6,22},{7,23},{8,24},{9,... | collective-permute-start | bytes 884744 | tf_op jit(solution)/shard_map/ppermute | solution.py:53
  248.7 15.3 %collective-permute-start.39 = (bf16[64,1536]{1,0:T(8,128)(2,1)S(1)}, bf16[64,1536]{1,0:T(8,128)(2,1)S(1)}, u32[]{:S(2)}, u32[]{:S(2)}) collective-permute-start(bf16[64,1536]{1,0:T(8,128)(2,1)S(1)} %get-tuple-element.227), channel_id=1, source_target_pairs={{0,16},{1,17},{2,18},{3,19},{4,20},{5,21},{6,22},{7,23},{8,24},{9,... | collective-permute-start | bytes 589832 | tf_op jit(solution)/shard_map/ppermute | solution.py:53
  248.9 15.1 %collective-permute-start.40 = (bf16[64,1536]{1,0:T(8,128)(2,1)S(1)}, bf16[64,1536]{1,0:T(8,128)(2,1)S(1)}, u32[]{:S(2)}, u32[]{:S(2)}) collective-permute-start(bf16[64,1536]{1,0:T(8,128)(2,1)S(1)} %get-tuple-element.228), channel_id=1, source_target_pairs={{0,24},{1,25},{2,26},{3,27},{4,28},{5,29},{6,30},{7,31},{8,16},{9,... | collective-permute-start | bytes 589832 | tf_op jit(solution)/shard_map/ppermute | solution.py:53
  (50 other events, 438.2 us)
